TPU v7x, 32 devices: a whole 2x2x4 slice. The times are simulated.
32 devices in a mesh: tm: 16 (over z, y, core), head: 2 (over x).
Axes of the slice: x: 2, y: 2, z: 4, core: 2. Of those that a mesh axis runs over, the one named last changes fastest.
Arguments:
- codes: int32 [16384, 8], P('tm'), may hold values from 0 to 1023
- tables: bfloat16 [8, 1024, 2048], P(None, None, 'head'), may hold values from -2.5 to 2.5
- conv_weight: bfloat16 [5, 2048, 2048], P(None, 'head'), may hold values from -0.0625 to 0.0625
- norm_gain: float32 [2048], replicated, may hold values from 0.1 to 1.9
- key_weight: bfloat16 [2048, 2048], P(None, 'head')
- value_weight: bfloat16 [2048, 2048], P(None, 'head'), may hold values from -0.125 to 0.125
- query_weight: bfloat16 [2048, 2048], P(None, 'head')
- latent_pos: int32 [512], replicated, may hold values from 0 to 4095, as said below
Outputs:
- attended: bfloat16 [512, 2048], P('tm', 'head')
Inputs may be any that keep to these rules, and one draw needn't show every extreme that they name: `latent_pos`: strictly increasing; holds every multiple of 256 and the last row 4095.
All inputs are finite; a program needn't handle non-finite values.
Results may differ from a plain program's by a relative error of at most 0.04.
The roundings to bfloat16 on the way count: a program that leaves them out, or rounds other values in their place, can miss the bound.
Values may be sent and summed in bfloat16 or wider, within the bound.
No kernel may reach another device: no remote copies, remote signals or barrier semaphores. Data moves between devices by JAX's collectives and lax.ppermute only.
A program may use at most 128 MiB of HBM per device.

v0:
```python
import math

import jax
import jax.numpy as jnp
from jax import lax
from jax.sharding import PartitionSpec as P

D = 2048
HEAD_DIM = 128
STRIDE = 4


def passed_along(value, axis, steps):
    count = lax.axis_size(axis)
    leading, last = (max(0, -steps), min(count, count - steps))
    return lax.ppermute(value, axis, [(source, source + steps) for source in range(leading, last)])


def on_device(
    codes, tables, conv_weight, norm_gain, key_weight, value_weight, query_weight, latent_pos
):
    frame_count = codes.shape[0]
    local_width = tables.shape[2]
    summed = jnp.zeros((frame_count, local_width), jnp.float32)
    for codebook in range(codes.shape[1]):
        summed = summed + jnp.take(tables[codebook], codes[:, codebook], axis=0).astype(jnp.float32)
    frames = summed.astype(jnp.bfloat16)
    taps = conv_weight.shape[0]
    lag_rows = taps - STRIDE
    row_count = frame_count // STRIDE
    previous = passed_along(frames[frame_count - lag_rows :], "tm", 1)
    padded = jnp.concatenate([previous, frames], 0)
    earlier = (
        padded[:frame_count]
        .reshape(row_count, STRIDE, local_width)[:, :lag_rows]
        .reshape(row_count, lag_rows * local_width)
    )
    latter = frames.reshape(row_count, STRIDE * local_width)
    window = jnp.concatenate([earlier, latter], 1)
    partial_value = jnp.dot(
        window,
        conv_weight.reshape(taps * local_width, conv_weight.shape[2]),
        preferred_element_type=jnp.float32,
    )
    portion = lax.psum_scatter(partial_value, "head", scatter_dimension=1, tiled=True).astype(
        jnp.bfloat16
    )
    widened = lax.all_gather(portion, "head", axis=1, tiled=True).astype(jnp.float32)
    scaled = (widened * norm_gain[None, :]).astype(jnp.bfloat16)
    key_acc = jnp.dot(scaled, key_weight, preferred_element_type=jnp.float32)
    value_acc = jnp.dot(scaled, value_weight, preferred_element_type=jnp.float32)
    query_acc = jnp.dot(scaled, query_weight, preferred_element_type=jnp.float32)
    squares = jnp.sum(widened * widened, 1)
    inverse = lax.rsqrt(squares / D + 1e-06)
    key_rows = (inverse[:, None] * key_acc).astype(jnp.bfloat16)
    value_rows = (inverse[:, None] * value_acc).astype(jnp.bfloat16)
    query_rows = (inverse[:, None] * query_acc).astype(jnp.bfloat16)
    first_row = lax.axis_index("tm") * row_count
    positions = first_row + jnp.arange(row_count, dtype=jnp.int32)
    selector = (latent_pos[:, None] == positions[None, :]).astype(jnp.bfloat16)
    selected = jnp.dot(selector, query_rows, preferred_element_type=jnp.float32)
    queries = lax.psum(selected.astype(jnp.bfloat16), "tm")
    latent_count = latent_pos.shape[0]
    group_heads = key_weight.shape[1] // HEAD_DIM
    query_three = queries.reshape(latent_count, group_heads, HEAD_DIM)
    key_three = key_rows.reshape(row_count, group_heads, HEAD_DIM)
    value_three = value_rows.reshape(row_count, group_heads, HEAD_DIM)
    scores = jnp.einsum(
        "lhd,rhd->hlr", query_three, key_three, preferred_element_type=jnp.float32
    ) * (1.0 / math.sqrt(HEAD_DIM))
    visible = (positions[None, :] <= latent_pos[:, None])[None, :, :]
    scores = jnp.where(visible, scores, -1e30)
    largest = jnp.max(scores, 2)
    weights = jnp.exp(scores - largest[:, :, None]) * visible.astype(jnp.float32)
    row_sums = jnp.sum(weights, 2)
    product = jnp.einsum(
        "hlr,rhd->lhd",
        weights.astype(jnp.bfloat16),
        value_three,
        preferred_element_type=jnp.float32,
    )
    product = product.reshape(latent_count, group_heads * HEAD_DIM)
    peaks = largest.T
    totals = row_sums.T
    peak_all = lax.pmax(peaks, "tm")
    factor = jnp.exp(peaks - peak_all)
    rescaled = product * jnp.repeat(factor, HEAD_DIM, axis=1)
    output_mine, total_mine = (
        lax.psum_scatter(
            rescaled.astype(jnp.bfloat16), "tm", scatter_dimension=0, tiled=True
        ).astype(jnp.float32),
        lax.psum_scatter(
            (totals * factor).astype(jnp.bfloat16), "tm", scatter_dimension=0, tiled=True
        ).astype(jnp.float32),
    )
    return (output_mine / jnp.repeat(total_mine, HEAD_DIM, axis=1)).astype(jnp.bfloat16)


def solution(mesh):
    placed = (
        P("tm", None),
        P(None, None, "head"),
        P(None, "head", None),
        P(),
        P(None, "head"),
        P(None, "head"),
        P(None, "head"),
        P(),
    )
    return jax.shard_map(
        on_device, mesh=mesh, in_specs=placed, out_specs=P("tm", "head"), check_vma=False
    )
```

profile of v0, /device:TPU:0, one launch (start us, length us, event | category | flops | bytes accessed | tf_op | source)
XLA Modules:
  0.0 457.3 jit_solution(12597088900499182918)
XLA Ops:
  6.5 1.1 fusion.50
  7.8 11.5 %slice_bitcast_fusion.7 = (bf16[1024,1024]{1,0:T(8,128)(2,1)}, bf16[1024,1024]{1,0:T(8,128)(2,1)}, bf16[1024,1024]{1,0:T(8,128)(2,1)}, bf16[1024,1024]{1,0:T(8,1...) fusion(bf16[8,1024,1024]{2,1,0:T(8,128)(2,1)} %param.11), kind=kLoop, calls=%fused_computation.37 | loop fusion | bytes 33554432 | tf_op jit(solution)/shard_map/squeeze | solution.py:26
  19.2 7.9 %gather_fusion.2 = bf16[1024,1024]{1,0:T(8,128)(2,1)} fusion(bf16[1024,1024]{1,0:T(8,128)(2,1)} %get-tuple-element.12, s32[1024]{0:T(1024)S(1)} %fusion.40), kind=kCustom, calls=%fused_computation.2.clone | custom fusion | bytes 4198400 | tf_op jit(solution)/shard_map/jit(_take)/gather | solution.py:26
  27.1 7.9 %gather_fusion.3 = bf16[1024,1024]{1,0:T(8,128)(2,1)} fusion(bf16[1024,1024]{1,0:T(8,128)(2,1)} %get-tuple-element.11, s32[1024]{0:T(1024)S(1)} %fusion.41), kind=kCustom, calls=%fused_computation.3.clone | custom fusion | bytes 4198400 | tf_op jit(solution)/shard_map/jit(_take)/gather | solution.py:26
  35.0 7.9 %gather_fusion.4 = bf16[1024,1024]{1,0:T(8,128)(2,1)} fusion(bf16[1024,1024]{1,0:T(8,128)(2,1)} %get-tuple-element.10, s32[1024]{0:T(1024)S(1)} %fusion.42), kind=kCustom, calls=%fused_computation.4.clone | custom fusion | bytes 4198400 | tf_op jit(solution)/shard_map/jit(_take)/gather | solution.py:26
  42.9 7.9 %gather_fusion.5 = bf16[1024,1024]{1,0:T(8,128)(2,1)} fusion(bf16[1024,1024]{1,0:T(8,128)(2,1)} %get-tuple-element.9, s32[1024]{0:T(1024)S(1)} %fusion.43), kind=kCustom, calls=%fused_computation.5.clone | custom fusion | bytes 4198400 | tf_op jit(solution)/shard_map/jit(_take)/gather | solution.py:26
  50.8 7.9 %gather_fusion.6 = bf16[1024,1024]{1,0:T(8,128)(2,1)} fusion(bf16[1024,1024]{1,0:T(8,128)(2,1)} %get-tuple-element.15, s32[1024]{0:T(1024)S(1)} %fusion.44), kind=kCustom, calls=%fused_computation.6.clone | custom fusion | bytes 4198400 | tf_op jit(solution)/shard_map/jit(_take)/gather | solution.py:26
  58.7 7.9 %gather_fusion.7 = bf16[1024,1024]{1,0:T(8,128)(2,1)} fusion(bf16[1024,1024]{1,0:T(8,128)(2,1)} %get-tuple-element.14, s32[1024]{0:T(1024)S(1)} %fusion.45), kind=kCustom, calls=%fused_computation.7.clone | custom fusion | bytes 4198400 | tf_op jit(solution)/shard_map/jit(_take)/gather | solution.py:26
  66.5 7.9 %gather_fusion = bf16[1024,1024]{1,0:T(8,128)(2,1)} fusion(bf16[1024,1024]{1,0:T(8,128)(2,1)} %get-tuple-element.8, s32[1024]{0:T(1024)S(1)} %fusion.38), kind=kCustom, calls=%fused_computation.clone | custom fusion | bytes 4198400 | tf_op jit(solution)/shard_map/jit(_take)/gather | solution.py:26
  74.4 5.3 %gather_fusion.1 = bf16[1024,1024]{1,0:T(8,128)(2,1)} fusion(bf16[1024,1024]{1,0:T(8,128)(2,1)S(1)} %get-tuple-element.13, s32[1024]{0:T(1024)S(1)} %fusion.39), kind=kCustom, calls=%fused_computation.1.clone | custom fusion | bytes 4198400 | tf_op jit(solution)/shard_map/jit(_take)/gather | solution.py:26
  79.8 8.3 %add_convert_fusion = bf16[1024,1024]{1,0:T(8,128)(2,1)S(1)} fusion(bf16[1024,1024]{1,0:T(8,128)(2,1)} %gather_fusion.7, bf16[1024,1024]{1,0:T(8,128)(2,1)} %gather_fusion.6, bf16[1024,1024]{1,0:T(8,128)(2,1)} %gather_fusion.5, bf16[1024,1024]{1,0:T(8,128)(2,1)} %gather_fusion.4, bf16[1024,1024]{1,0:T(8,128)(2,1)} %gather_fusion.3, ...), kind=kLoop, calls=%fused_computation.10 | loop fusion | flops 25165824 | bytes 18882560 | tf_op jit(solution)/shard_map/convert_element_type | solution.py:27
  88.1 2.6 collective-permute-start
  90.6 2.6 reshape.99
  93.2 1.9 pad_maximum_fusion
  95.1 2.7 reshape.97
  97.8 0.7 slice.93
  98.6 0.2 copy.41
  98.7 0.7 copy-done
  99.4 11.2 %fusion.3 = f32[256,2048]{1,0:T(8,128)} fusion(bf16[5120,2048]{1,0:T(8,128)(2,1)} %bitcast.87, bf16[256,4096]{1,0:T(8,128)(2,1)S(1)} %copy-done, bf16[256,1024]{1,0:T(8,128)(2,1)S(1)} %bitcast.67), kind=kOutput, calls=%fused_computation.16 | convolution fusion | flops 5373952000 | bytes 25690112 | tf_op jit(solution)/shard_map/dot_general | solution.py:40
  110.7 0.0 reduce-scatter.6.cloned.1.call-update
  110.7 0.0 all-gather.2.cloned.1.call-start
  110.7 34.5 %reduce-scatter.6.cloned.1.call-done = f32[256,1024]{1,0:T(8,128)} async-done(((f32[256,2048]{1,0:T(8,128)}), f32[256,1024]{1,0:T(8,128)}) %reduce-scatter.6.cloned.1.call-update) | async-done | bytes 1048592 | tf_op jit(solution)/shard_map/reduce_scatter | solution.py:45
  145.3 2.1 convert_element_type.87
  147.4 0.0 all-reduce.2.cloned.1.call-start
  147.5 0.2 broadcast_compare_fusion
  147.7 21.2 %all-gather.2.cloned.1.call-done = bf16[256,2048]{1,0:T(8,128)(2,1)} async-done(((bf16[256,1024]{1,0:T(8,128)(2,1)}), bf16[256,2048]{1,0:T(8,128)(2,1)}) %all-gather.2.cloned.1.call-update) | async-done | bytes 1048592 | tf_op jit(solution)/shard_map/all_gather | solution.py:48
  168.9 1.5 fusion.7
  170.4 4.0 fusion.19
  174.5 1.2 copy.40
  175.7 0.0 reduce-scatter.10.cloned.1.call-start
  175.7 0.2 copy-done.1
  175.9 3.4 fusion.20
  179.4 0.2 copy.24
  179.6 3.6 fusion.23
  183.1 86.5 %all-reduce.2.cloned.1.call-done = bf16[512,8,128]{2,0,1:T(8,128)(2,1)} async-done(((bf16[512,8,128]{2,0,1:T(8,128)(2,1)}), bf16[512,8,128]{2,0,1:T(8,128)(2,1)}) %all-reduce.2.cloned.1.call-update) | async-done | bytes 1048592 | tf_op jit(solution)/shard_map/psum | solution.py:62
  269.7 4.0 fusion
  273.7 58.4 %pmax.7 = f32[512,8]{0,1:T(8,128)S(1)} all-reduce(f32[512,8]{0,1:T(8,128)S(1)} %bitcast.70), channel_id=1, replica_groups=mesh['tm'=16,'head'=2] {'tm'}, use_global_device_ids=true, to_apply=%region_4.6 | all-reduce | flops 4096 | bytes 32768 | tf_op jit(solution)/shard_map/pmax | solution.py:85
  332.1 3.2 fusion.1
  335.3 0.8 copy.25
  336.1 0.0 reduce-scatter.8.cloned.1.call-start
  336.2 3.6 fusion.11
  339.8 1.3 copy.21
  341.1 48.0 %reduce-scatter.10.cloned.1.call-done = bf16[32,8]{1,0:T(8,128)(2,1)} async-done(((bf16[512,8]{1,0:T(8,128)(2,1)}), bf16[32,8]{1,0:T(8,128)(2,1)}) %reduce-scatter.10.cloned.1.call-update) | async-done | bytes 528
  389.2 0.8 copy.26
  389.9 0.1 copy.22
  390.0 59.2 %reduce-scatter.8.cloned.1.call-done = bf16[32,1024]{1,0:T(8,128)(2,1)} async-done(((bf16[512,1024]{1,0:T(8,128)(2,1)}), bf16[32,1024]{1,0:T(8,128)(2,1)}) %reduce-scatter.8.cloned.1.call-update) | async-done | bytes 65552 | tf_op jit(solution)/shard_map/reduce_scatter | solution.py:89
  449.2 0.1 broadcast_in_dim.40
  449.3 1.5 fusion.36
  (28 shorter events, 0.2 us)
Async XLA Ops:
  6.5 138.8 %reduce-scatter.6.cloned.1.call-start = ((), (), s32[]{:S(2)}) async-start(), calls=%async_computation.3 | async-start | bytes 3145728 | tf_op jit(solution)/shard_map/reduce_scatter | solution.py:45
  88.1 5.1 %collective-permute-start = (bf16[1,1024]{1,0:T(2,128)(2,1)S(1)}, bf16[1,1024]{1,0:T(2,128)(2,1)S(1)}, u32[]{:S(2)}, u32[]{:S(2)}) collective-permute-start(bf16[1,1024]{1,0:T(2,128)(2,1)S(1)} %slice.92), channel_id=1, source_target_pairs={{0,2},{2,4},{4,6},{6,8},{8,10},{10,12},{12,14},{14,16},{16,18},{18... | collective-permute-start | bytes 6152 | tf_op jit(solution)/shard_map/ppermute | solution.py:16
  97.8 1.6 copy-start
  110.7 36.8 %copy-start.2 = (s32[512]{0:T(512)S(1)}, s32[512]{0:T(512)}, u32[]{:S(2)}) copy-start(s32[512]{0:T(512)} %param.17) | copy-start | bytes 6148
  110.7 59.7 %copy-start.3 = (f32[2048]{0:T(1024)S(1)}, f32[2048]{0:T(1024)}, u32[]{:S(2)}) copy-start(f32[2048]{0:T(1024)} %param.13) | copy-start | bytes 24580
  110.7 58.2 %all-gather.2.cloned.1.call-start = ((), (), s32[]{:S(2)}) async-start(), calls=%async_computation.4 | async-start | bytes 1572864 | tf_op jit(solution)/shard_map/all_gather | solution.py:48
  147.4 122.3 %all-reduce.2.cloned.1.call-start = ((), (), s32[]{:S(2)}) async-start(), calls=%async_computation.5 | async-start | bytes 2097152 | tf_op jit(solution)/shard_map/psum | solution.py:62
  174.4 1.5 copy-start.1
  175.7 213.5 %reduce-scatter.10.cloned.1.call-start = ((), (), s32[]{:S(2)}) async-start(), calls=%async_computation.7 | async-start | bytes 139264
  336.1 113.1 %reduce-scatter.8.cloned.1.call-start = ((), (), s32[]{:S(2)}) async-start(), calls=%async_computation.6 | async-start | bytes 1114112 | tf_op jit(solution)/shard_map/reduce_scatter | solution.py:89
Sparse Core Ops, SparseCore 0:
  110.8 34.4 reduce-scatter.5
  147.5 21.2 all-gather.1
  175.8 93.8 all-reduce.1
  336.2 52.8 reduce-scatter.9
  392.6 56.5 reduce-scatter.7
where the time goes:
time: 458 us; the launch traced here: 457 us
  waiting for transfers between devices  250 us (55%)
  local copies, waits for them, and re-layouts  84.5 us (18%)
  blocking collectives  58.4 us (13%)
  matrix products  29.9 us (7%)
  other arithmetic  18.7 us (4%)
  between operations  13.4 us (3%)
    psum x1, waiting for transfers between devices, on_device(): queries = lax.psum(selected.astype(jnp.bfloat16), 'tm')  86.5 us
    gather x8, local copies, waits for them, and re-layouts, on_device(): jnp.take(tables[codebook], codes[:, codebook], axis=0).astype(jnp.float32)  60.5 us
    reduce_scatter x1, waiting for transfers between devices, on_device(): lax.psum_scatter(rescaled.astype(jnp.bfloat16), 'tm', scatter_dimension=0...  59.2 us
    pmax x1, blocking collectives, on_device(): peak_all = lax.pmax(peaks, 'tm')  58.4 us
    unnamed x6, waiting for transfers between devices  48.1 us
    reduce_scatter x1, waiting for transfers between devices, on_device(): lax.psum_scatter(partial_value, 'head', scatter_dimension=1, tiled=True)  34.5 us
    all_gather x1, waiting for transfers between devices, on_device(): lax.all_gather(portion, 'head', axis=1, tiled=True).astype(jnp.float32)  21.2 us
    squeeze x1, local copies, waits for them, and re-layouts, on_device(): tables[codebook]  11.5 us
  transfers between devices with their start and end apart: 6, of which 5 were waited for; matrix products, arithmetic and copies ran while one was open for 3% of the time, Pallas kernels for 0%

commit v1 on v0

v1 whole, which is shorter than its diff:
```python
import functools
import math

import jax
import jax.numpy as jnp
from jax import lax
from jax.experimental import pallas as pl
from jax.experimental.pallas import tpu as pltpu
from jax.sharding import PartitionSpec as P

HEAD_DIM = 128
STRIDE = 4
PAD = 16
LANES = 128
VMEM = pltpu.VMEM
HIDDEN = -1e30


def exchange_stages(count):
    stages, remaining = [], count
    while remaining > 2:
        factor = 4 if remaining % 4 == 0 and remaining // 4 >= 2 else 2
        step = remaining // factor
        stages.append([step * k for k in range(1, factor)])
        remaining = step
    return stages


def swapped(value, axis, offset):
    count = lax.axis_size(axis)
    return lax.ppermute(value, axis, [(i, i ^ offset) for i in range(count)])


def gathered(value, axis, stages):
    offsets = [0]
    for stage in stages:
        value = jnp.concatenate([value] + [swapped(value, axis, d) for d in stage], 0)
        offsets = [o ^ d for d in [0] + stage for o in offsets]
    return value, offsets


def row_tiles(rows):
    parts = max(1, round(rows / 208))
    unit = PAD * parts
    padded = -(-rows // unit) * unit
    return padded, padded // parts


def embed_conv(codes, tables, conv_weight, rows, extra, tile, first):
    total = codes.shape[0]
    books, vocab, width = tables.shape
    taps, _, features = conv_weight.shape
    span = rows + extra
    block = min(512, features)

    def body(codes_ref, tables_in, conv_in, part_ref, *rest):
        if first:
            tables_ref, conv_ref, frames_ref, lag_ref, table_sem, conv_sem = rest
            table_copies = [
                pltpu.make_async_copy(tables_in.at[c], tables_ref.at[c], table_sem.at[c])
                for c in range(books)
            ]
            conv_copies = [
                pltpu.make_async_copy(conv_in.at[k], conv_ref.at[k], conv_sem.at[k])
                for k in range(taps)
            ]
            for copy in table_copies:
                copy.start()
        else:
            tables_ref, conv_ref = tables_in, conv_in
            frames_ref, lag_ref = rest

        def one_tile(r, arrive):
            found = None
            for c in range(books):
                if arrive:
                    table_copies[c].wait()
                    if c < taps:
                        conv_copies[c].start()
                hot = codes_ref[r, c : c + 1] == lax.broadcasted_iota(jnp.int32, (tile, vocab), 1)
                got = jnp.dot(
                    hot.astype(jnp.float32).astype(jnp.bfloat16),
                    tables_ref[c],
                    preferred_element_type=jnp.float32,
                )
                found = got if found is None else found + got
            frames_ref[r, :] = found.astype(jnp.bfloat16)

        begin = 0
        if first:
            one_tile(pl.ds(0, tile), True)
            begin = 1
        if total // tile > begin:

            def step(t, carry):
                one_tile(pl.ds(pl.multiple_of(t * tile, tile), tile), False)
                return carry

            lax.fori_loop(begin, total // tile, step, 0)

        last = frames_ref[pl.ds((STRIDE - 1) * span, rows), :].astype(jnp.float32)
        before = frames_ref[pl.ds(STRIDE * span, PAD), :].astype(jnp.float32)[0:1]
        moved = pltpu.roll(last, 1, 0)
        line = lax.broadcasted_iota(jnp.int32, (rows, width), 0)
        lag_ref[pl.ds(0, rows), :] = jnp.where(line == 0, before, moved).astype(jnp.bfloat16)
        if extra:
            lag_ref[pl.ds(rows, extra), :] = frames_ref[pl.ds(STRIDE * span + PAD, extra), :]
        if first:
            for copy in conv_copies:
                copy.wait()
        for column in range(0, features, block):
            found = jnp.dot(
                lag_ref[...],
                conv_ref[0, :, column : column + block],
                preferred_element_type=jnp.float32,
            )
            for k in range(1, taps):
                found += jnp.dot(
                    frames_ref[pl.ds((k - 1) * span, span), :],
                    conv_ref[k, :, column : column + block],
                    preferred_element_type=jnp.float32,
                )
            part_ref[:, column : column + block] = found.astype(jnp.bfloat16)

    vmem = pl.BlockSpec(memory_space=VMEM)
    held = pl.BlockSpec(memory_space=pl.ANY) if first else vmem
    part = jax.ShapeDtypeStruct((span, features), jnp.bfloat16)
    scratch = [VMEM((total, width), jnp.bfloat16), VMEM((span, width), jnp.bfloat16)]
    if first:
        scratch += [pltpu.SemaphoreType.DMA((books,)), pltpu.SemaphoreType.DMA((taps,))]
    return pl.pallas_call(
        body,
        in_specs=[vmem, held, held],
        out_specs=[vmem] * 3 if first else vmem,
        out_shape=[
            part,
            VMEM(tables.shape, tables.dtype),
            VMEM(conv_weight.shape, conv_weight.dtype),
        ]
        if first
        else part,
        scratch_shapes=scratch,
        compiler_params=pltpu.CompilerParams(vmem_limit_bytes=16 << 20),
        cost_estimate=pl.CostEstimate(
            flops=2 * total * books * vocab * width + 2 * span * taps * width * features,
            bytes_accessed=36 << 20 if first else 4 << 20,
            transcendentals=0,
        ),
        name="embed_conv",
    )(codes, tables, conv_weight)


def summed_rows(part_refs, gain_ref, where):
    total = part_refs[0][where, :].astype(jnp.float32)
    for ref in part_refs[1:]:
        total = total + ref[where, :].astype(jnp.float32)
    conv_out = total.astype(jnp.bfloat16).astype(jnp.float32)
    mean = jnp.sum(conv_out * conv_out, 1, keepdims=True) / conv_out.shape[1]
    inverse = lax.rsqrt(mean + 1e-06)
    return (conv_out * gain_ref[...]).astype(jnp.bfloat16), inverse


def project(parts, gain, weights, begin, rows, name):
    features, columns = weights[0].shape
    count = len(parts)
    block = min(512, columns)

    def body(*refs):
        part_refs, gain_ref = refs[:count], refs[count]
        weight_refs = refs[count + 1 : count + 1 + len(weights)]
        out_ref = refs[count + 1 + len(weights)]
        scaled, inverse = summed_rows(part_refs, gain_ref, pl.ds(begin, rows))
        for i, weight_ref in enumerate(weight_refs):
            for column in range(0, columns, block):
                found = jnp.dot(
                    scaled,
                    weight_ref[:, column : column + block],
                    preferred_element_type=jnp.float32,
                )
                at = i * columns + column
                out_ref[:, at : at + block] = (inverse * found).astype(jnp.bfloat16)

    vmem = pl.BlockSpec(memory_space=VMEM)
    return pl.pallas_call(
        body,
        in_specs=[vmem] * (count + 1 + len(weights)),
        out_specs=vmem,
        out_shape=jax.ShapeDtypeStruct((rows, columns * len(weights)), jnp.bfloat16),
        compiler_params=pltpu.CompilerParams(vmem_limit_bytes=16 << 20),
        cost_estimate=pl.CostEstimate(
            flops=2 * rows * features * columns * len(weights),
            bytes_accessed=2 * features * columns * len(weights),
            transcendentals=0,
        ),
        name=name,
    )(*parts, gain, *weights)


def attend(place, slots, queries, keys_values, latent_rows):
    latents, width = queries.shape
    owners = slots.shape[0]
    each = latents // owners
    heads = width // HEAD_DIM
    rows = [kv.shape[0] for kv in keys_values]
    all_rows = sum(rows)

    def body(place_ref, slots_ref, q_ref, pos_ref, *rest):
        kv_refs = rest[: len(rows)]
        out_ref, query_ref = rest[len(rows) :]
        for owner in range(owners):
            at = pl.multiple_of(slots_ref[owner] * each, each)
            query_ref[pl.ds(owner * each, each), :] = q_ref[pl.ds(at, each), :]
        lane = lax.broadcasted_iota(jnp.int32, (latents, LANES), 1)
        stats = jnp.zeros((latents, LANES), jnp.float32)
        line = lax.broadcasted_iota(jnp.int32, (latents, all_rows), 1)
        base, start = jnp.zeros((latents, all_rows), jnp.int32), 0
        for i, count in enumerate(rows):
            base = jnp.where(line >= start, place_ref[i] - start, base)
            start += count
        visible = (line + base) <= pos_ref[...]
        for head in range(heads):
            here = slice(head * HEAD_DIM, (head + 1) * HEAD_DIM)
            there = slice(width + head * HEAD_DIM, width + (head + 1) * HEAD_DIM)
            keys = jnp.concatenate([ref[:, here] for ref in kv_refs], 0)
            values = jnp.concatenate([ref[:, there] for ref in kv_refs], 0)
            scores = lax.dot_general(
                query_ref[:, here],
                keys,
                (((1,), (1,)), ((), ())),
                preferred_element_type=jnp.float32,
            ) * (1.0 / math.sqrt(HEAD_DIM))
            scores = jnp.where(visible, scores, HIDDEN)
            largest = jnp.max(scores, 1, keepdims=True)
            weights = jnp.where(visible, jnp.exp(scores - largest), 0.0)
            total = jnp.sum(weights, 1, keepdims=True)
            product = jnp.dot(
                weights.astype(jnp.bfloat16), values, preferred_element_type=jnp.float32
            )
            out_ref[:, here] = product.astype(jnp.bfloat16)
            for i, value in enumerate((largest, total)):
                for piece in range(3):
                    part = value.astype(jnp.bfloat16).astype(jnp.float32)
                    stats = jnp.where(lane == (3 * i + piece) * heads + head, part, stats)
                    value = value - part
        out_ref[:, width : width + LANES] = stats.astype(jnp.bfloat16)

    vmem = pl.BlockSpec(memory_space=VMEM)
    smem = pl.BlockSpec(memory_space=pltpu.SMEM)
    return pl.pallas_call(
        body,
        in_specs=[smem, smem] + [vmem] * (2 + len(rows)),
        out_specs=vmem,
        out_shape=jax.ShapeDtypeStruct((latents, width + LANES), jnp.bfloat16),
        scratch_shapes=[VMEM((latents, width), jnp.bfloat16)],
        compiler_params=pltpu.CompilerParams(vmem_limit_bytes=24 << 20),
        cost_estimate=pl.CostEstimate(
            flops=4 * latents * all_rows * width,
            bytes_accessed=4 << 20,
            transcendentals=latents * all_rows * heads,
        ),
        name="attend",
    )(place, slots, queries, latent_rows, *keys_values)


def merge(partials, owners):
    each = partials.shape[0] // owners
    width = partials.shape[1] - LANES
    heads = width // HEAD_DIM

    def body(in_ref, out_ref):
        largest, total = [], []
        for owner in range(owners):
            stats = in_ref[pl.ds(owner * each, each), width:].astype(jnp.float32)
            column = lambda i: stats[:, i * heads : (i + 1) * heads]
            largest.append(column(0) + column(1) + column(2))
            total.append(column(3) + column(4) + column(5))
        top = functools.reduce(jnp.maximum, largest)
        factors = [jnp.exp(value - top) for value in largest]
        bottom = sum(f * t for f, t in zip(factors, total))
        for head in range(heads):
            here = slice(head * HEAD_DIM, (head + 1) * HEAD_DIM)
            found = jnp.zeros((each, HEAD_DIM), jnp.float32)
            for owner in range(owners):
                value = in_ref[pl.ds(owner * each, each), here].astype(jnp.float32)
                found += factors[owner][:, head : head + 1] * value
            out_ref[:, here] = (found / bottom[:, head : head + 1]).astype(jnp.bfloat16)

    vmem = pl.BlockSpec(memory_space=VMEM)
    return pl.pallas_call(
        body,
        in_specs=[vmem],
        out_specs=vmem,
        out_shape=jax.ShapeDtypeStruct((each, width), jnp.bfloat16),
        name="merge",
    )(partials)


def on_device(
    codes, tables, conv_weight, norm_gain, key_weight, value_weight, query_weight, latent_pos
):
    shards = lax.axis_size("tm")
    heads_axis = lax.axis_size("head")
    me = lax.axis_index("tm")
    frame_count, books = codes.shape
    taps = conv_weight.shape[0]
    lag = taps - STRIDE
    row_count = frame_count // STRIDE
    mine = latent_pos.shape[0] // shards
    stages = exchange_stages(shards)

    all_codes, offsets = gathered(codes.astype(jnp.int16), "tm", stages + [[1]])
    place_of = jnp.asarray([offsets.index(i) for i in range(shards)], jnp.int32)
    my_rows = lax.dynamic_slice(latent_pos, (me * mine,), (mine,))
    wanted = STRIDE * my_rows[None, :] - lag + jnp.arange(taps, dtype=jnp.int32)[:, None]
    wanted = jnp.concatenate([wanted.reshape(-1), (me * frame_count - 1)[None]])
    safe = jnp.maximum(wanted, 0)
    line = place_of[(safe // frame_count) ^ me] * frame_count + safe % frame_count
    fetched = jnp.take(all_codes, line, axis=0).astype(jnp.int32)
    fetched = jnp.where(wanted[:, None] >= 0, fetched, -1)
    window_codes = fetched[: taps * mine].reshape(taps, mine, books)
    phases = codes.reshape(row_count, STRIDE, books).transpose(1, 0, 2)

    gain = norm_gain[None, :]
    cuts = [(0, row_count // 4, mine), (row_count // 4, row_count * 3 // 8, 0)]
    cuts += [(row_count * 5 // 8, row_count * 3 // 8, 0)]
    held = (tables, conv_weight)
    partner_parts = []
    chunks = []
    queries = None
    for index, (begin, rows, extra) in enumerate(cuts):
        pieces = []
        for phase in range(STRIDE):
            pieces.append(phases[phase, begin : begin + rows])
            if extra:
                pieces.append(window_codes[lag + phase])
        before = fetched[taps * mine :] if begin == 0 else phases[STRIDE - 1, begin - 1 : begin]
        pieces += [before, jnp.full((PAD - 1, books), -1, jnp.int32)]
        if extra:
            pieces.append(window_codes[0])
        used = STRIDE * (rows + extra) + PAD + extra
        padded, tile = row_tiles(used)
        if padded > used:
            pieces.append(jnp.full((padded - used, books), -1, jnp.int32))
        chunk_codes = jnp.concatenate(pieces, 0)
        made = embed_conv(chunk_codes, *held, rows, extra, tile, index == 0)
        if index == 0:
            part, *held = made
        else:
            part = made
        if extra:
            window_parts = [part[rows:]]
            window_parts += [swapped(part[rows:], "head", d) for d in range(1, heads_axis)]
            queries = project(window_parts, gain, [query_weight], 0, extra, "queries")
            part = part[:rows]
        parts = [part] + [swapped(part, "head", d) for d in range(1, heads_axis)]
        chunks.append(project(parts, gain, [key_weight, value_weight], 0, rows, "keys_values"))
    all_queries, offsets = gathered(queries, "tm", stages)
    others = [swapped(chunk, "tm", 1) for chunk in chunks]

    owners = shards // 2
    slot_of = jnp.asarray([offsets.index(2 * i) for i in range(owners)], jnp.int32)
    slots = slot_of[jnp.arange(owners, dtype=jnp.int32) ^ (me // 2)]
    place = jnp.stack(
        [me * row_count + cut[0] for cut in cuts] + [(me ^ 1) * row_count + cut[0] for cut in cuts]
    ).astype(jnp.int32)
    by_core = latent_pos.reshape(owners, 2, mine)
    latent_rows = lax.dynamic_index_in_dim(by_core, me % 2, 1, False).reshape(owners * mine, 1)
    partials = attend(place, slots, all_queries, chunks + others, latent_rows)
    groups = [[2 * i + core for i in range(owners)] for core in range(2)]
    partials = lax.all_to_all(
        partials, "tm", 0, 0, axis_index_groups=groups, tiled=True
    )
    return merge(partials, owners)


def solution(mesh):
    placed = (
        P("tm", None),
        P(None, None, "head"),
        P(None, "head", None),
        P(),
        P(None, "head"),
        P(None, "head"),
        P(None, "head"),
        P(),
    )
    return jax.shard_map(
        on_device, mesh=mesh, in_specs=placed, out_specs=P("tm", "head"), check_vma=False
    )
```

time: 458 us -> 138 us (0.30)
  waiting for transfers between devices: 250 us -> 9.87 us
  Pallas kernels: 0 us -> 49.1 us
  local copies, waits for them, and re-layouts: 84.5 us -> 37.1 us
  blocking collectives: 58.4 us -> 21.1 us
  matrix products: 29.9 us -> 0 us
  other arithmetic: 18.7 us -> 1.98 us
  starting transfers between devices: 2.75 us -> 18.3 us
  between operations: 13.4 us -> 0.37 us
    reduce_scatter x2 -> x0, waiting for transfers between devices: 93.8 us -> none  [the longest x1 59.2 us: on_device(): lax.psum_scatter(rescaled.astype(jnp.bfloat16), 'tm', scatter_dimension=0...]
    psum x1 -> x0, waiting for transfers between devices: 86.5 us -> none  [on_device(): queries = lax.psum(selected.astype(jnp.bfloat16), 'tm')]
    pmax x1 -> x0, blocking collectives: 58.4 us -> none  [on_device(): peak_all = lax.pmax(peaks, 'tm')]
    gather x8 -> x2, local copies, waits for them, and re-layouts: 60.5 us -> 4.71 us  [the longest x1 3.41 us: on_device(): fetched = jnp.take(all_codes, line, axis=0).astype(jnp.int32)]
    pallas_call x0 -> x9, Pallas kernels: none -> 49.1 us  [the longest x3 37.6 us: embed_conv(): pl.pallas_call(body, in_specs=[vmem, held, held], out_specs=[vmem] * 3 if...]
    unnamed x6 -> x0, waiting for transfers between devices: 48.1 us -> none
    dot_general x6 -> x0, matrix products: 29.9 us -> none  [the longest x1 11.2 us: on_device(): jnp.dot(window, conv_weight.reshape(taps * local_width, conv_weight.shape...]
    unnamed x11 -> x25, local copies, waits for them, and re-layouts: 2.56 us -> 26.6 us
  transfers between devices with their start and end apart: 6 -> 16, of which waited for: 5 -> 7; matrix products, arithmetic and copies ran while one was open for 3% -> 4% of each run, Pallas kernels for 0% -> 20%
where the time goes in v1:
time: 138 us
  Pallas kernels  49.1 us (36%)
  local copies, waits for them, and re-layouts  37.1 us (27%)
  blocking collectives  21.1 us (15%)
  starting transfers between devices  18.3 us (13%)
  waiting for transfers between devices  9.87 us (7%)
  other arithmetic  1.98 us (1%)
    pallas_call x3, Pallas kernels, embed_conv(): pl.pallas_call(body, in_specs=[vmem, held, held], out_specs=[vmem] * 3 if...  37.6 us
    unnamed x25, local copies, waits for them, and re-layouts  26.6 us
    all_to_all x1, blocking collectives, on_device(): lax.all_to_all(partials, 'tm', 0, 0, axis_index_groups=groups, tiled=True)  21.1 us
    ppermute x16, starting transfers between devices, swapped(): return lax.ppermute(value, axis, [(i, i ^ offset) for i in range(count)])  18.3 us
    ppermute x16, waiting for transfers between devices, swapped(): return lax.ppermute(value, axis, [(i, i ^ offset) for i in range(count)])  9.87 us
    pallas_call x4, Pallas kernels, project(): pl.pallas_call(body, in_specs=[vmem] * (count + 1 + len(weights)), out_sp...  5.45 us
    concatenate x4, local copies, waits for them, and re-layouts, gathered(): jnp.concatenate([value] + [swapped(value, axis, d) for d in stage], 0)  4.16 us
    pallas_call x1, Pallas kernels, attend(): pl.pallas_call(body, in_specs=[smem, smem] + [vmem] * (2 + len(rows)), ou...  3.94 us
  transfers between devices with their start and end apart: 16, of which 7 were waited for; matrix products, arithmetic and copies ran while one was open for 4% of the time, Pallas kernels for 20%

profile of v1, /device:TPU:0, one launch (start us, length us, event | category | flops | bytes accessed | tf_op | source)
XLA Modules:
  0.0 137.8 jit_solution(3837262131647065491)
XLA Ops:
  0.0 0.8 constant_dynamic-update-slice_fusion.4
  0.8 5.1 %collective-permute-start.2 = (s16[1024,8]{0,1:T(8,128)(2,1)S(1)}, s16[1024,8]{0,1:T(8,128)(2,1)S(1)}, u32[]{:S(2)}, u32[]{:S(2)}) collective-permute-start(s16[1024,8]{0,1:T(8,128)(2,1)S(1)} %get-tuple-element.25), channel_id=1, source_target_pairs={{0,24},{2,26},{4,28},{6,30},{8,16},{10,18},{12,20},{14,22},{16,8},... | collective-permute-start | bytes 49160 | tf_op jit(solution)/shard_map/ppermute | solution.py:31
  5.8 0.6 collective-permute-start
  6.4 0.8 multiply_add_fusion
  7.2 0.1 concatenate.57
  7.3 1.0 copy.41
  8.4 0.1 compare_select_fusion.2
  8.6 0.1 compare_and_fusion
  8.7 1.7 %collective-permute-done.1 = s16[1024,8]{0,1:T(8,128)(2,1)S(1)} collective-permute-done((s16[1024,8]{0,1:T(8,128)(2,1)S(1)}, s16[1024,8]{0,1:T(8,128)(2,1)S(1)}, u32[]{:S(2)}, u32[]{:S(2)}) %collective-permute-start.1) | collective-permute-done | bytes 16416 | tf_op jit(solution)/shard_map/ppermute | solution.py:31
  10.5 1.6 %collective-permute-start.3 = (s16[4096,8]{0,1:T(8,128)(2,1)S(1)}, s16[4096,8]{0,1:T(8,128)(2,1)S(1)}, u32[]{:S(2)}, u32[]{:S(2)}) collective-permute-start(s16[4096,8]{0,1:T(8,128)(2,1)S(1)} %pad_add_fusion), channel_id=1, source_target_pairs={{0,4},{2,6},{4,0},{6,2},{8,12},{10,14},{12,8},{14,10},{16,20},{18,... | collective-permute-start | bytes 196616 | tf_op jit(solution)/shard_map/ppermute | solution.py:31
  12.1 2.7 %collective-permute-done.3 = s16[4096,8]{0,1:T(8,128)(2,1)S(1)} collective-permute-done((s16[4096,8]{0,1:T(8,128)(2,1)S(1)}, s16[4096,8]{0,1:T(8,128)(2,1)S(1)}, u32[]{:S(2)}, u32[]{:S(2)}) %collective-permute-start.3) | collective-permute-done | bytes 65568 | tf_op jit(solution)/shard_map/ppermute | solution.py:31
  14.9 0.8 reshape.196
  15.7 0.1 reshape.282.pos_ref
  15.9 1.3 gather_fusion
  17.2 0.1 concatenate.67.codes_ref
  17.3 0.1 concatenate.66.codes_ref
  17.5 0.1 stack.27.place_ref
  17.6 4.1 %copy.43 = s16[16384,8]{1,0:T(8,128)(2,1)} copy(s16[16384,8]{0,1:T(8,128)(2,1)S(1)} %constant_dynamic-update-slice_fusion.5) | data formatting | bytes 524288 | tf_op jit(solution)/shard_map/concatenate | solution.py:37
  21.7 3.4 %gather_fusion.1 = s16[161,8]{1,0:T(8,128)(2,1)S(1)} fusion(s16[16384,8]{1,0:T(8,128)(2,1)} %copy.43, s32[1024]{0:T(1024)S(1)} %pad_clamp_fusion), kind=kCustom, calls=%fused_computation.1 | custom fusion | bytes 5796 | tf_op jit(solution)/shard_map/jit(_take)/gather | solution.py:318
  25.1 0.1 convert_select_fusion
  25.3 0.1 concatenate.63.codes_ref
  25.4 15.6 %embed_conv.3 = (bf16[96,2048]{1,0:T(8,128)(2,1)S(1)}, bf16[8,1024,1024]{2,1,0:T(8,128)(2,1)S(1)}, bf16[5,1024,2048]{2,1,0:T(8,128)(2,1)S(1)}) custom-call(s32[448,8]{1,0:T(8,128)S(1)} %concatenate.63.codes_ref, bf16[8,1024,1024]{2,1,0:T(8,128)(2,1)} %tables_in.1, bf16[5,1024,2048]{2,1,0:T(8,128)(2,1)} %conv_in.1), custom_call_target="tpu_custom_call" | custom-call | flops 9529458688 | bytes 37748736 | tf_op jit(solution)/shard_map/embed_conv/pallas_call | solution.py:131
  41.0 7.0 %copy-done = bf16[5,1024,2048]{2,1,0:T(8,128)(2,1)} copy-done((bf16[5,1024,2048]{2,1,0:T(8,128)(2,1)}, bf16[5,1024,2048]{2,1,0:T(8,128)(2,1)S(1)}, u32[]{:S(2)}) %copy-start) | copy-done | bytes 20971544
  48.0 5.8 %copy-done.2 = bf16[8,1024,1024]{2,1,0:T(8,128)(2,1)} copy-done((bf16[8,1024,1024]{2,1,0:T(8,128)(2,1)}, bf16[8,1024,1024]{2,1,0:T(8,128)(2,1)S(1)}, u32[]{:S(2)}) %copy-start.2) | copy-done | bytes 16777240
  53.9 1.6 %collective-permute-start.5 = (bf16[32,2048]{1,0:T(8,128)(2,1)S(1)}, bf16[32,2048]{1,0:T(8,128)(2,1)S(1)}, u32[]{:S(2)}, u32[]{:S(2)}) collective-permute-start(bf16[32,2048]{1,0:T(8,128)(2,1)S(1)} %slice.86.refs_0_), channel_id=1, source_target_pairs={{0,1},{1,0},{2,3},{3,2},{4,5},{5,4},{6,7},{7,6},{8,9},{9,8},{10,11... | collective-permute-start | bytes 393224 | tf_op jit(solution)/shard_map/ppermute | solution.py:31
  55.4 7.0 %copy-done.1 = bf16[5,1024,2048]{2,1,0:T(8,128)(2,1)S(1)} copy-done((bf16[5,1024,2048]{2,1,0:T(8,128)(2,1)S(1)}, bf16[5,1024,2048]{2,1,0:T(8,128)(2,1)}, u32[]{:S(2)}) %copy-start.1) | copy-done | bytes 20971544
  62.4 5.8 %copy-done.3 = bf16[8,1024,1024]{2,1,0:T(8,128)(2,1)S(1)} copy-done((bf16[8,1024,1024]{2,1,0:T(8,128)(2,1)S(1)}, bf16[8,1024,1024]{2,1,0:T(8,128)(2,1)}, u32[]{:S(2)}) %copy-start.3) | copy-done | bytes 16777240
  68.2 10.9 %embed_conv.4.refs_0_ = bf16[96,2048]{1,0:T(8,128)(2,1)S(1)} custom-call(s32[416,8]{1,0:T(8,128)S(1)} %concatenate.66.codes_ref, bf16[8,1024,1024]{2,1,0:T(8,128)(2,1)S(1)} %copy-done.3, bf16[5,1024,2048]{2,1,0:T(8,128)(2,1)S(1)} %copy-done.1), custom_call_target="tpu_custom_call" | custom-call | flops 8992587776 | bytes 4194304 | tf_op jit(solution)/shard_map/embed_conv/pallas_call | solution.py:131
  79.1 0.6 collective-permute-start.11
  79.7 11.1 %embed_conv.5.refs_0_ = bf16[96,2048]{1,0:T(8,128)(2,1)S(1)} custom-call(s32[416,8]{1,0:T(8,128)S(1)} %concatenate.67.codes_ref, bf16[8,1024,1024]{2,1,0:T(8,128)(2,1)S(1)} %copy-done.3, bf16[5,1024,2048]{2,1,0:T(8,128)(2,1)S(1)} %copy-done.1), custom_call_target="tpu_custom_call" | custom-call | flops 8992587776 | bytes 4194304 | tf_op jit(solution)/shard_map/embed_conv/pallas_call | solution.py:131
  90.8 1.5 %collective-permute-start.12 = (bf16[96,2048]{1,0:T(8,128)(2,1)S(1)}, bf16[96,2048]{1,0:T(8,128)(2,1)S(1)}, u32[]{:S(2)}, u32[]{:S(2)}) collective-permute-start(bf16[96,2048]{1,0:T(8,128)(2,1)S(1)} %embed_conv.5.refs_0_), channel_id=1, source_target_pairs={{0,1},{1,0},{2,3},{3,2},{4,5},{5,4},{6,7},{7,6},{8,9},{9,8},{10,11... | collective-permute-start | bytes 1179656 | tf_op jit(solution)/shard_map/ppermute | solution.py:31
  92.4 0.8 queries.1
  93.2 2.1 %collective-permute-start.8 = (bf16[32,1024]{1,0:T(8,128)(2,1)S(1)}, bf16[32,1024]{1,0:T(8,128)(2,1)S(1)}, u32[]{:S(2)}, u32[]{:S(2)}) collective-permute-start(bf16[32,1024]{1,0:T(8,128)(2,1)S(1)} %queries.1), channel_id=1, source_target_pairs={{0,24},{2,26},{4,28},{6,30},{8,16},{10,18},{12,20},{14,22},{16,8},... | collective-permute-start | bytes 196616 | tf_op jit(solution)/shard_map/ppermute | solution.py:31
  95.3 2.3 %collective-permute-start.6 = (bf16[32,1024]{1,0:T(8,128)(2,1)S(1)}, bf16[32,1024]{1,0:T(8,128)(2,1)S(1)}, u32[]{:S(2)}, u32[]{:S(2)}) collective-permute-start(bf16[32,1024]{1,0:T(8,128)(2,1)S(1)} %queries.1), channel_id=1, source_target_pairs={{0,8},{2,10},{4,12},{6,14},{8,0},{10,2},{12,4},{14,6},{16,24},{18,... | collective-permute-start | bytes 196616 | tf_op jit(solution)/shard_map/ppermute | solution.py:31
  97.6 1.9 %collective-permute-done.8 = bf16[32,1024]{1,0:T(8,128)(2,1)S(1)} collective-permute-done((bf16[32,1024]{1,0:T(8,128)(2,1)S(1)}, bf16[32,1024]{1,0:T(8,128)(2,1)S(1)}, u32[]{:S(2)}, u32[]{:S(2)}) %collective-permute-start.8) | collective-permute-done | bytes 65568 | tf_op jit(solution)/shard_map/ppermute | solution.py:31
  99.5 0.5 collective-permute-start.10
  100.0 1.6 %collective-permute-done.7 = bf16[32,1024]{1,0:T(8,128)(2,1)S(1)} collective-permute-done((bf16[32,1024]{1,0:T(8,128)(2,1)S(1)}, bf16[32,1024]{1,0:T(8,128)(2,1)S(1)}, u32[]{:S(2)}, u32[]{:S(2)}) %collective-permute-start.7) | collective-permute-done | bytes 65568 | tf_op jit(solution)/shard_map/ppermute | solution.py:31
  101.6 1.6 %collective-permute-start.9 = (bf16[128,1024]{1,0:T(8,128)(2,1)S(1)}, bf16[128,1024]{1,0:T(8,128)(2,1)S(1)}, u32[]{:S(2)}, u32[]{:S(2)}) collective-permute-start(bf16[128,1024]{1,0:T(8,128)(2,1)S(1)} %pad_maximum_fusion), channel_id=1, source_target_pairs={{0,4},{2,6},{4,0},{6,2},{8,12},{10,14},{12,8},{14,10},{16,20},{18,... | collective-permute-start | bytes 786440 | tf_op jit(solution)/shard_map/ppermute | solution.py:31
  103.3 1.5 %keys_values.4.rest_1_ = bf16[96,2048]{1,0:T(8,128)(2,1)S(1)} custom-call(bf16[96,2048]{1,0:T(8,128)(2,1)S(1)} %embed_conv.4.refs_0_, bf16[96,2048]{1,0:T(8,128)(2,1)S(1)} %collective-permute-done.11.refs_1_, f32[1,2048]{1,0:T(1,128)S(1)} %bitcast.50, bf16[2048,1024]{1,0:T(8,128)(2,1)S(1)} %copy-done.4, bf16[2048,1024]{1,0:T(8,128)(2,1)S(1)} %copy-done.5), custom_call_target="tpu_custom_call" | custom-call | flops 805306368 | bytes 8388608 | tf_op jit(solution)/shard_map/keys_values/pallas_call | solution.py:184
  104.9 1.5 %keys_values.5.rest_2_ = bf16[96,2048]{1,0:T(8,128)(2,1)S(1)} custom-call(bf16[96,2048]{1,0:T(8,128)(2,1)S(1)} %embed_conv.5.refs_0_, bf16[96,2048]{1,0:T(8,128)(2,1)S(1)} %collective-permute-done.12.refs_1_, f32[1,2048]{1,0:T(1,128)S(1)} %bitcast.51, bf16[2048,1024]{1,0:T(8,128)(2,1)S(1)} %copy-done.4, bf16[2048,1024]{1,0:T(8,128)(2,1)S(1)} %copy-done.5), custom_call_target="tpu_custom_call" | custom-call | flops 805306368 | bytes 8388608 | tf_op jit(solution)/shard_map/keys_values/pallas_call | solution.py:184
  106.4 0.6 collective-permute-start.15
  107.0 0.4 collective-permute-done.10.refs_1_
  107.4 1.6 %keys_values.3.rest_0_ = bf16[64,2048]{1,0:T(8,128)(2,1)S(1)} custom-call(bf16[64,2048]{1,0:T(8,128)(2,1)S(1)} %slice.87.refs_0_, bf16[64,2048]{1,0:T(8,128)(2,1)S(1)} %collective-permute-done.10.refs_1_, f32[1,2048]{1,0:T(1,128)S(1)} %bitcast.52, bf16[2048,1024]{1,0:T(8,128)(2,1)S(1)} %copy-done.4, bf16[2048,1024]{1,0:T(8,128)(2,1)S(1)} %copy-done.5), custom_call_target="tpu_custom_call" | custom-call | flops 536870912 | bytes 8388608 | tf_op jit(solution)/shard_map/keys_values/pallas_call | solution.py:184
  109.1 0.7 collective-permute-done.9
  109.9 0.7 collective-permute-done.13.rest_3_
  110.6 3.9 %attend.1 = bf16[256,1152]{1,0:T(8,128)(2,1)S(1)} custom-call(s32[6]{0:T(128)S(1)} %stack.27.place_ref, s32[8]{0:T(128)S(1)} %gather_fusion, bf16[256,1024]{1,0:T(8,128)(2,1)S(1)} %constant_dynamic-update-slice_fusion.11.q_ref, s32[256,1]{1,0:T(8,128)S(1)} %reshape.282.pos_ref, bf16[64,2048]{1,0:T(8,128)(2,1)S(1)} %keys_values.3.rest_0_, ...), custom_call_target="tpu_custom_call" | custom-call | flops 536870912 | bytes 4194304 | tf_op jit(solution)/shard_map/attend/pallas_call | solution.py:249
  114.5 21.1 %all_to_all.11 = bf16[8,32,1152]{2,1,0:T(8,128)(2,1)} all-to-all(bf16[8,32,1152]{2,1,0:T(8,128)(2,1)S(1)} %bitcast.48), channel_id=1, replica_groups={{0,4,8,12,16,20,24,28},{2,6,10,14,18,22,26,30},{1,5,9,13,17,21,25,29},{..., dimensions={0} | all-to-all | bytes 1179648 | tf_op jit(solution)/shard_map/all_to_all | solution.py:370
  135.6 2.2 %merge.1 = bf16[32,1024]{1,0:T(8,128)(2,1)} custom-call(bf16[256,1152]{1,0:T(8,128)(2,1)} %bitcast.53), custom_call_target="tpu_custom_call" | custom-call | tf_op jit(solution)/shard_map/merge/pallas_call | solution.py:289
  (57 shorter events, 0.7 us)
Async XLA Ops:
  0.8 8.0 %collective-permute-start.2 = (s16[1024,8]{0,1:T(8,128)(2,1)S(1)}, s16[1024,8]{0,1:T(8,128)(2,1)S(1)}, u32[]{:S(2)}, u32[]{:S(2)}) collective-permute-start(s16[1024,8]{0,1:T(8,128)(2,1)S(1)} %get-tuple-element.25), channel_id=1, source_target_pairs={{0,24},{2,26},{4,28},{6,30},{8,16},{10,18},{12,20},{14,22},{16,8},... | collective-permute-start | bytes 49160 | tf_op jit(solution)/shard_map/ppermute | solution.py:31
  5.8 4.6 %collective-permute-start.1 = (s16[1024,8]{0,1:T(8,128)(2,1)S(1)}, s16[1024,8]{0,1:T(8,128)(2,1)S(1)}, u32[]{:S(2)}, u32[]{:S(2)}) collective-permute-start(s16[1024,8]{0,1:T(8,128)(2,1)S(1)} %get-tuple-element.25), channel_id=1, source_target_pairs={{0,16},{2,18},{4,20},{6,22},{8,24},{10,26},{12,28},{14,30},{16,0},... | collective-permute-start | bytes 49160 | tf_op jit(solution)/shard_map/ppermute | solution.py:31
  5.8 4.6 %collective-permute-start = (s16[1024,8]{0,1:T(8,128)(2,1)S(1)}, s16[1024,8]{0,1:T(8,128)(2,1)S(1)}, u32[]{:S(2)}, u32[]{:S(2)}) collective-permute-start(s16[1024,8]{0,1:T(8,128)(2,1)S(1)} %get-tuple-element.25), channel_id=1, source_target_pairs={{0,8},{2,10},{4,12},{6,14},{8,0},{10,2},{12,4},{14,6},{16,24},{18,... | collective-permute-start | bytes 49160 | tf_op jit(solution)/shard_map/ppermute | solution.py:31
  10.5 4.3 %collective-permute-start.3 = (s16[4096,8]{0,1:T(8,128)(2,1)S(1)}, s16[4096,8]{0,1:T(8,128)(2,1)S(1)}, u32[]{:S(2)}, u32[]{:S(2)}) collective-permute-start(s16[4096,8]{0,1:T(8,128)(2,1)S(1)} %pad_add_fusion), channel_id=1, source_target_pairs={{0,4},{2,6},{4,0},{6,2},{8,12},{10,14},{12,8},{14,10},{16,20},{18,... | collective-permute-start | bytes 196616 | tf_op jit(solution)/shard_map/ppermute | solution.py:31
  14.8 2.7 %collective-permute-start.4 = (s16[8192,8]{0,1:T(8,128)(2,1)S(1)}, s16[8192,8]{0,1:T(8,128)(2,1)S(1)}, u32[]{:S(2)}, u32[]{:S(2)}) collective-permute-start(s16[8192,8]{0,1:T(8,128)(2,1)S(1)} %get-tuple-element.44), channel_id=1, source_target_pairs={{0,2},{2,0},{4,6},{6,4},{8,10},{10,8},{12,14},{14,12},{16,18},{18,... | collective-permute-start | bytes 393224 | tf_op jit(solution)/shard_map/ppermute | solution.py:31
  41.0 7.0 %copy-start = (bf16[5,1024,2048]{2,1,0:T(8,128)(2,1)}, bf16[5,1024,2048]{2,1,0:T(8,128)(2,1)S(1)}, u32[]{:S(2)}) copy-start(bf16[5,1024,2048]{2,1,0:T(8,128)(2,1)S(1)} %get-tuple-element.10.conv_in) | copy-start | bytes 62914564
  48.0 5.8 %copy-start.2 = (bf16[8,1024,1024]{2,1,0:T(8,128)(2,1)}, bf16[8,1024,1024]{2,1,0:T(8,128)(2,1)S(1)}, u32[]{:S(2)}) copy-start(bf16[8,1024,1024]{2,1,0:T(8,128)(2,1)S(1)} %get-tuple-element.9.tables_in) | copy-start | bytes 50331652
  53.9 38.5 %collective-permute-start.5 = (bf16[32,2048]{1,0:T(8,128)(2,1)S(1)}, bf16[32,2048]{1,0:T(8,128)(2,1)S(1)}, u32[]{:S(2)}, u32[]{:S(2)}) collective-permute-start(bf16[32,2048]{1,0:T(8,128)(2,1)S(1)} %slice.86.refs_0_), channel_id=1, source_target_pairs={{0,1},{1,0},{2,3},{3,2},{4,5},{5,4},{6,7},{7,6},{8,9},{9,8},{10,11... | collective-permute-start | bytes 393224 | tf_op jit(solution)/shard_map/ppermute | solution.py:31
  55.4 7.0 %copy-start.1 = (bf16[5,1024,2048]{2,1,0:T(8,128)(2,1)S(1)}, bf16[5,1024,2048]{2,1,0:T(8,128)(2,1)}, u32[]{:S(2)}) copy-start(bf16[5,1024,2048]{2,1,0:T(8,128)(2,1)} %copy-done) | copy-start | bytes 62914564
  62.4 5.8 %copy-start.3 = (bf16[8,1024,1024]{2,1,0:T(8,128)(2,1)S(1)}, bf16[8,1024,1024]{2,1,0:T(8,128)(2,1)}, u32[]{:S(2)}) copy-start(bf16[8,1024,1024]{2,1,0:T(8,128)(2,1)} %copy-done.2) | copy-start | bytes 50331652
  79.0 13.3 %copy-start.6 = (bf16[2048,1024]{1,0:T(8,128)(2,1)S(1)}, bf16[2048,1024]{1,0:T(8,128)(2,1)}, u32[]{:S(2)}) copy-start(bf16[2048,1024]{1,0:T(8,128)(2,1)} %refs_3_.4) | copy-start | bytes 12582916
  79.0 13.3 %copy-start.7 = (f32[2048]{0:T(1024)S(1)}, f32[2048]{0:T(1024)}, u32[]{:S(2)}) copy-start(f32[2048]{0:T(1024)} %param.13) | copy-start | bytes 24580
  79.1 24.2 %collective-permute-start.11 = (bf16[96,2048]{1,0:T(8,128)(2,1)S(1)}, bf16[96,2048]{1,0:T(8,128)(2,1)S(1)}, u32[]{:S(2)}, u32[]{:S(2)}) collective-permute-start(bf16[96,2048]{1,0:T(8,128)(2,1)S(1)} %embed_conv.4.refs_0_), channel_id=1, source_target_pairs={{0,1},{1,0},{2,3},{3,2},{4,5},{5,4},{6,7},{7,6},{8,9},{9,8},{10,11... | collective-permute-start | bytes 1179656 | tf_op jit(solution)/shard_map/ppermute | solution.py:31
  79.7 23.6 %copy-start.5 = (bf16[2048,1024]{1,0:T(8,128)(2,1)S(1)}, bf16[2048,1024]{1,0:T(8,128)(2,1)}, u32[]{:S(2)}) copy-start(bf16[2048,1024]{1,0:T(8,128)(2,1)} %refs_4_.5) | copy-start | bytes 12582916
  90.8 12.5 %copy-start.4 = (bf16[2048,1024]{1,0:T(8,128)(2,1)S(1)}, bf16[2048,1024]{1,0:T(8,128)(2,1)}, u32[]{:S(2)}) copy-start(bf16[2048,1024]{1,0:T(8,128)(2,1)} %refs_3_.7) | copy-start | bytes 12582916
  90.8 14.1 %collective-permute-start.12 = (bf16[96,2048]{1,0:T(8,128)(2,1)S(1)}, bf16[96,2048]{1,0:T(8,128)(2,1)S(1)}, u32[]{:S(2)}, u32[]{:S(2)}) collective-permute-start(bf16[96,2048]{1,0:T(8,128)(2,1)S(1)} %embed_conv.5.refs_0_), channel_id=1, source_target_pairs={{0,1},{1,0},{2,3},{3,2},{4,5},{5,4},{6,7},{7,6},{8,9},{9,8},{10,11... | collective-permute-start | bytes 1179656 | tf_op jit(solution)/shard_map/ppermute | solution.py:31
  93.2 6.3 %collective-permute-start.8 = (bf16[32,1024]{1,0:T(8,128)(2,1)S(1)}, bf16[32,1024]{1,0:T(8,128)(2,1)S(1)}, u32[]{:S(2)}, u32[]{:S(2)}) collective-permute-start(bf16[32,1024]{1,0:T(8,128)(2,1)S(1)} %queries.1), channel_id=1, source_target_pairs={{0,24},{2,26},{4,28},{6,30},{8,16},{10,18},{12,20},{14,22},{16,8},... | collective-permute-start | bytes 196616 | tf_op jit(solution)/shard_map/ppermute | solution.py:31
  95.3 6.3 %collective-permute-start.7 = (bf16[32,1024]{1,0:T(8,128)(2,1)S(1)}, bf16[32,1024]{1,0:T(8,128)(2,1)S(1)}, u32[]{:S(2)}, u32[]{:S(2)}) collective-permute-start(bf16[32,1024]{1,0:T(8,128)(2,1)S(1)} %queries.1), channel_id=1, source_target_pairs={{0,16},{2,18},{4,20},{6,22},{8,24},{10,26},{12,28},{14,30},{16,0},... | collective-permute-start | bytes 196616 | tf_op jit(solution)/shard_map/ppermute | solution.py:31
  95.3 6.3 %collective-permute-start.6 = (bf16[32,1024]{1,0:T(8,128)(2,1)S(1)}, bf16[32,1024]{1,0:T(8,128)(2,1)S(1)}, u32[]{:S(2)}, u32[]{:S(2)}) collective-permute-start(bf16[32,1024]{1,0:T(8,128)(2,1)S(1)} %queries.1), channel_id=1, source_target_pairs={{0,8},{2,10},{4,12},{6,14},{8,0},{10,2},{12,4},{14,6},{16,24},{18,... | collective-permute-start | bytes 196616 | tf_op jit(solution)/shard_map/ppermute | solution.py:31
  99.5 7.9 %collective-permute-start.10 = (bf16[64,2048]{1,0:T(8,128)(2,1)S(1)}, bf16[64,2048]{1,0:T(8,128)(2,1)S(1)}, u32[]{:S(2)}, u32[]{:S(2)}) collective-permute-start(bf16[64,2048]{1,0:T(8,128)(2,1)S(1)} %slice.87.refs_0_), channel_id=1, source_target_pairs={{0,1},{1,0},{2,3},{3,2},{4,5},{5,4},{6,7},{7,6},{8,9},{9,8},{10,11... | collective-permute-start | bytes 786440 | tf_op jit(solution)/shard_map/ppermute | solution.py:31
  101.6 8.2 %collective-permute-start.9 = (bf16[128,1024]{1,0:T(8,128)(2,1)S(1)}, bf16[128,1024]{1,0:T(8,128)(2,1)S(1)}, u32[]{:S(2)}, u32[]{:S(2)}) collective-permute-start(bf16[128,1024]{1,0:T(8,128)(2,1)S(1)} %pad_maximum_fusion), channel_id=1, source_target_pairs={{0,4},{2,6},{4,0},{6,2},{8,12},{10,14},{12,8},{14,10},{16,20},{18,... | collective-permute-start | bytes 786440 | tf_op jit(solution)/shard_map/ppermute | solution.py:31
  104.8 5.8 %collective-permute-start.14 = (bf16[96,2048]{1,0:T(8,128)(2,1)S(1)}, bf16[96,2048]{1,0:T(8,128)(2,1)S(1)}, u32[]{:S(2)}, u32[]{:S(2)}) collective-permute-start(bf16[96,2048]{1,0:T(8,128)(2,1)S(1)} %keys_values.4.rest_1_), channel_id=1, source_target_pairs={{0,2},{2,0},{4,6},{6,4},{8,10},{10,8},{12,14},{14,12},{16,18},{18,... | collective-permute-start | bytes 1179656 | tf_op jit(solution)/shard_map/ppermute | solution.py:31
  106.4 4.2 %collective-permute-start.15 = (bf16[96,2048]{1,0:T(8,128)(2,1)S(1)}, bf16[96,2048]{1,0:T(8,128)(2,1)S(1)}, u32[]{:S(2)}, u32[]{:S(2)}) collective-permute-start(bf16[96,2048]{1,0:T(8,128)(2,1)S(1)} %keys_values.5.rest_2_), channel_id=1, source_target_pairs={{0,2},{2,0},{4,6},{6,4},{8,10},{10,8},{12,14},{14,12},{16,18},{18,... | collective-permute-start | bytes 1179656 | tf_op jit(solution)/shard_map/ppermute | solution.py:31
  109.0 1.6 %collective-permute-start.13 = (bf16[64,2048]{1,0:T(8,128)(2,1)S(1)}, bf16[64,2048]{1,0:T(8,128)(2,1)S(1)}, u32[]{:S(2)}, u32[]{:S(2)}) collective-permute-start(bf16[64,2048]{1,0:T(8,128)(2,1)S(1)} %keys_values.3.rest_0_), channel_id=1, source_target_pairs={{0,2},{2,0},{4,6},{6,4},{8,10},{10,8},{12,14},{14,12},{16,18},{18,... | collective-permute-start | bytes 786440 | tf_op jit(solution)/shard_map/ppermute | solution.py:31

commit v2 on v1

--- a/solution.py
+++ b/solution.py
@@ -14,6 +14,8 @@
 LANES = 128
 VMEM = pltpu.VMEM
 HIDDEN = -1e30
+EMBED_LIMIT = 4 << 20
+PROJECT_LIMIT = 8 << 20
 
 
 def exchange_stages(count):
@@ -32,11 +34,12 @@
 
 
 def gathered(value, axis, stages):
-    offsets = [0]
+    offsets, pieces = [0], [value]
     for stage in stages:
-        value = jnp.concatenate([value] + [swapped(value, axis, d) for d in stage], 0)
+        whole = jnp.concatenate(pieces, 0)
+        pieces = pieces + [swapped(whole, axis, d) for d in stage]
         offsets = [o ^ d for d in [0] + stage for o in offsets]
-    return value, offsets
+    return pieces, offsets
 
 
 def row_tiles(rows):
@@ -46,16 +49,26 @@
     return padded, padded // parts
 
 
-def embed_conv(codes, tables, conv_weight, rows, extra, tile, first):
-    total = codes.shape[0]
-    books, vocab, width = tables.shape
-    taps, _, features = conv_weight.shape
+def embed_conv(phases, table_source, conv_source, cut, windows, first, keep):
+    begin, rows = cut
+    books, vocab, width = table_source.shape
+    taps, _, features = conv_source.shape
+    extra = 0 if windows is None else (windows[1].shape[0] - PAD) // taps
     span = rows + extra
+    total, tile = row_tiles((STRIDE * span) + PAD + extra)
     block = min(512, features)
 
-    def body(codes_ref, tables_in, conv_in, part_ref, *rest):
+    def body(*refs):
+        phases_ref, refs = refs[0], refs[1:]
+        if extra:
+            (all_ref, line_ref), refs = refs[:2], refs[2:]
+        tables_in, conv_in, part_ref, *refs = refs
         if first:
-            tables_ref, conv_ref, frames_ref, lag_ref, table_sem, conv_sem = rest
+            *refs, table_sem, conv_sem = refs
+            if keep:
+                tables_ref, conv_ref, *refs = refs
+            else:
+                *refs, tables_ref, conv_ref = refs
             table_copies = [
                 pltpu.make_async_copy(tables_in.at[c], tables_ref.at[c], table_sem.at[c])
                 for c in range(books)
@@ -68,7 +81,42 @@
                 copy.start()
         else:
             tables_ref, conv_ref = tables_in, conv_in
-            frames_ref, lag_ref = rest
+        codes_ref, frames_ref, lag_ref = refs
+
+        for phase in range(STRIDE):
+            codes_ref[pl.ds(phase * span, rows), :] = phases_ref[phase, pl.ds(begin, rows), :]
+        tail = STRIDE * span
+        if extra:
+            line = line_ref[...]
+            count = line.shape[0]
+            groups, lanes = all_ref.shape[0], all_ref.shape[1] // books
+            wide = all_ref[...].astype(jnp.int32)
+            pick = (line // lanes == lax.broadcasted_iota(jnp.int32, (count, groups), 1)).astype(
+                jnp.float32
+            ).astype(jnp.bfloat16)
+            low = (wide % 32).astype(jnp.float32).astype(jnp.bfloat16)
+            high = (wide // 32).astype(jnp.float32).astype(jnp.bfloat16)
+            found = jnp.dot(pick, high, preferred_element_type=jnp.float32) * 32.0 + jnp.dot(
+                pick, low, preferred_element_type=jnp.float32
+            )
+            lane = lax.broadcasted_iota(jnp.int32, (count, lanes), 1)
+            fetched = jnp.zeros((count, books), jnp.int32)
+            column = lax.broadcasted_iota(jnp.int32, (count, books), 1)
+            for c in range(books):
+                one = jnp.where(lane == line % lanes, found[:, c * lanes : (c + 1) * lanes], 0.0)
+                one = jnp.sum(one, 1, keepdims=True).astype(jnp.int32)
+                fetched = jnp.where(column == c, one, fetched)
+            fetched = jnp.where(line >= 0, fetched, -1)
+            codes_ref[pl.ds(tail, PAD + extra), :] = fetched[: PAD + extra]
+            for k in range(1, taps):
+                codes_ref[pl.ds((k - 1) * span + rows, extra), :] = fetched[
+                    PAD + k * extra : PAD + (k + 1) * extra
+                ]
+        else:
+            codes_ref[pl.ds(tail, PAD), :] = phases_ref[STRIDE - 1, pl.ds(begin - PAD, PAD), :]
+        used = tail + PAD + extra
+        if total > used:
+            codes_ref[pl.ds(used, total - used), :] = jnp.full((total - used, books), -1, jnp.int32)
 
         def one_tile(r, arrive):
             found = None
@@ -86,25 +134,25 @@
                 found = got if found is None else found + got
             frames_ref[r, :] = found.astype(jnp.bfloat16)
 
-        begin = 0
+        ready = 0
         if first:
             one_tile(pl.ds(0, tile), True)
-            begin = 1
-        if total // tile > begin:
+            ready = 1
+        if total // tile > ready:
 
             def step(t, carry):
                 one_tile(pl.ds(pl.multiple_of(t * tile, tile), tile), False)
                 return carry
 
-            lax.fori_loop(begin, total // tile, step, 0)
+            lax.fori_loop(ready, total // tile, step, 0)
 
         last = frames_ref[pl.ds((STRIDE - 1) * span, rows), :].astype(jnp.float32)
-        before = frames_ref[pl.ds(STRIDE * span, PAD), :].astype(jnp.float32)[0:1]
+        before = frames_ref[pl.ds(tail, PAD), :].astype(jnp.float32)[PAD - 1 :]
         moved = pltpu.roll(last, 1, 0)
         line = lax.broadcasted_iota(jnp.int32, (rows, width), 0)
         lag_ref[pl.ds(0, rows), :] = jnp.where(line == 0, before, moved).astype(jnp.bfloat16)
         if extra:
-            lag_ref[pl.ds(rows, extra), :] = frames_ref[pl.ds(STRIDE * span + PAD, extra), :]
+            lag_ref[pl.ds(rows, extra), :] = frames_ref[pl.ds(tail + PAD, extra), :]
         if first:
             for copy in conv_copies:
                 copy.wait()
@@ -125,29 +173,33 @@
     vmem = pl.BlockSpec(memory_space=VMEM)
     held = pl.BlockSpec(memory_space=pl.ANY) if first else vmem
     part = jax.ShapeDtypeStruct((span, features), jnp.bfloat16)
-    scratch = [VMEM((total, width), jnp.bfloat16), VMEM((span, width), jnp.bfloat16)]
+    scratch = [
+        VMEM((total, books), jnp.int32),
+        VMEM((total, width), jnp.bfloat16),
+        VMEM((span, width), jnp.bfloat16),
+    ]
+    big = [VMEM(held.shape, held.dtype) for held in (table_source, conv_source)]
+    limit = EMBED_LIMIT
     if first:
+        if not keep:
+            scratch += big
+            limit += 2 * (table_source.size + conv_source.size)
         scratch += [pltpu.SemaphoreType.DMA((books,)), pltpu.SemaphoreType.DMA((taps,))]
+    operands = [phases] + list(windows or ())
     return pl.pallas_call(
         body,
-        in_specs=[vmem, held, held],
-        out_specs=[vmem] * 3 if first else vmem,
-        out_shape=[
-            part,
-            VMEM(tables.shape, tables.dtype),
-            VMEM(conv_weight.shape, conv_weight.dtype),
-        ]
-        if first
-        else part,
+        in_specs=[vmem] * len(operands) + [held, held],
+        out_specs=[vmem] * 3 if keep else [vmem],
+        out_shape=[part] + big if keep else [part],
         scratch_shapes=scratch,
-        compiler_params=pltpu.CompilerParams(vmem_limit_bytes=16 << 20),
+        compiler_params=pltpu.CompilerParams(vmem_limit_bytes=limit),
         cost_estimate=pl.CostEstimate(
             flops=2 * total * books * vocab * width + 2 * span * taps * width * features,
             bytes_accessed=36 << 20 if first else 4 << 20,
             transcendentals=0,
         ),
         name="embed_conv",
-    )(codes, tables, conv_weight)
+    )(*operands, table_source, conv_source)
 
 
 def summed_rows(part_refs, gain_ref, where):
@@ -160,16 +212,23 @@
     return (conv_out * gain_ref[...]).astype(jnp.bfloat16), inverse
 
 
-def project(parts, gain, weights, begin, rows, name):
+def project(groups, gain, weights, name):
     features, columns = weights[0].shape
-    count = len(parts)
     block = min(512, columns)
+    operands = [part for group in groups for part in group[0]]
+    rows = sum(group[2] for group in groups)
+    count = len(operands)
 
     def body(*refs):
         part_refs, gain_ref = refs[:count], refs[count]
         weight_refs = refs[count + 1 : count + 1 + len(weights)]
         out_ref = refs[count + 1 + len(weights)]
-        scaled, inverse = summed_rows(part_refs, gain_ref, pl.ds(begin, rows))
+        pieces, at = [], 0
+        for parts, begin, size in groups:
+            pieces.append(summed_rows(part_refs[at : at + len(parts)], gain_ref, pl.ds(begin, size)))
+            at += len(parts)
+        scaled = jnp.concatenate([piece[0] for piece in pieces], 0)
+        inverse = jnp.concatenate([piece[1] for piece in pieces], 0)
         for i, weight_ref in enumerate(weight_refs):
             for column in range(0, columns, block):
                 found = jnp.dot(
@@ -186,35 +245,39 @@
         in_specs=[vmem] * (count + 1 + len(weights)),
         out_specs=vmem,
         out_shape=jax.ShapeDtypeStruct((rows, columns * len(weights)), jnp.bfloat16),
-        compiler_params=pltpu.CompilerParams(vmem_limit_bytes=16 << 20),
+        compiler_params=pltpu.CompilerParams(vmem_limit_bytes=PROJECT_LIMIT),
         cost_estimate=pl.CostEstimate(
             flops=2 * rows * features * columns * len(weights),
             bytes_accessed=2 * features * columns * len(weights),
             transcendentals=0,
         ),
         name=name,
-    )(*parts, gain, *weights)
-
-
-def attend(place, slots, queries, keys_values, latent_rows):
-    latents, width = queries.shape
-    owners = slots.shape[0]
+    )(*operands, gain, *weights)
+
+
+def attend(place, owner_of, queries, keys_values, runs, latent_rows):
+    width = queries[0].shape[1]
+    owners = owner_of.shape[0]
+    latents = latent_rows.shape[0]
     each = latents // owners
     heads = width // HEAD_DIM
-    rows = [kv.shape[0] for kv in keys_values]
-    all_rows = sum(rows)
-
-    def body(place_ref, slots_ref, q_ref, pos_ref, *rest):
-        kv_refs = rest[: len(rows)]
-        out_ref, query_ref = rest[len(rows) :]
-        for owner in range(owners):
-            at = pl.multiple_of(slots_ref[owner] * each, each)
-            query_ref[pl.ds(owner * each, each), :] = q_ref[pl.ds(at, each), :]
+    all_rows = sum(runs)
+    pieces = len(queries)
+
+    def body(place_ref, owner_ref, pos_ref, *rest):
+        q_refs, kv_refs = rest[:pieces], rest[pieces:-2]
+        out_ref, query_ref = rest[-2:]
+        block = 0
+        for q_ref in q_refs:
+            for i in range(q_ref.shape[0] // each):
+                at = pl.multiple_of(owner_ref[block] * each, each)
+                query_ref[pl.ds(at, each), :] = q_ref[pl.ds(i * each, each), :]
+                block += 1
         lane = lax.broadcasted_iota(jnp.int32, (latents, LANES), 1)
         stats = jnp.zeros((latents, LANES), jnp.float32)
-        line = lax.broadcasted_iota(jnp.int32, (latents, all_rows), 1)
-        base, start = jnp.zeros((latents, all_rows), jnp.int32), 0
-        for i, count in enumerate(rows):
+        line = lax.broadcasted_iota(jnp.int32, (1, all_rows), 1)
+        base, start = jnp.zeros((1, all_rows), jnp.int32), 0
+        for i, count in enumerate(runs):
             base = jnp.where(line >= start, place_ref[i] - start, base)
             start += count
         visible = (line + base) <= pos_ref[...]
@@ -248,7 +311,7 @@
     smem = pl.BlockSpec(memory_space=pltpu.SMEM)
     return pl.pallas_call(
         body,
-        in_specs=[smem, smem] + [vmem] * (2 + len(rows)),
+        in_specs=[smem, smem] + [vmem] * (1 + pieces + len(keys_values)),
         out_specs=vmem,
         out_shape=jax.ShapeDtypeStruct((latents, width + LANES), jnp.bfloat16),
         scratch_shapes=[VMEM((latents, width), jnp.bfloat16)],
@@ -259,7 +322,7 @@
             transcendentals=latents * all_rows * heads,
         ),
         name="attend",
-    )(place, slots, queries, latent_rows, *keys_values)
+    )(place, owner_of, latent_rows, *queries, *keys_values)
 
 
 def merge(partials, owners):
@@ -308,67 +371,50 @@
     mine = latent_pos.shape[0] // shards
     stages = exchange_stages(shards)
 
-    all_codes, offsets = gathered(codes.astype(jnp.int16), "tm", stages + [[1]])
-    place_of = jnp.asarray([offsets.index(i) for i in range(shards)], jnp.int32)
+    lines = codes.astype(jnp.int16).reshape(frame_count // LANES, LANES, books)
+    lines = lines.transpose(0, 2, 1).reshape(frame_count // LANES, books * LANES)
+    pieces, offsets = gathered(lines, "tm", stages + [[1]])
+    all_lines = jnp.concatenate(pieces, 0)
     my_rows = lax.dynamic_slice(latent_pos, (me * mine,), (mine,))
     wanted = STRIDE * my_rows[None, :] - lag + jnp.arange(taps, dtype=jnp.int32)[:, None]
-    wanted = jnp.concatenate([wanted.reshape(-1), (me * frame_count - 1)[None]])
-    safe = jnp.maximum(wanted, 0)
-    line = place_of[(safe // frame_count) ^ me] * frame_count + safe % frame_count
-    fetched = jnp.take(all_codes, line, axis=0).astype(jnp.int32)
-    fetched = jnp.where(wanted[:, None] >= 0, fetched, -1)
-    window_codes = fetched[: taps * mine].reshape(taps, mine, books)
+    wanted = jnp.concatenate(
+        [jnp.full((PAD - 1,), -1, jnp.int32), (me * frame_count - 1)[None], wanted.reshape(-1)]
+    )
+    holder = jnp.maximum(wanted, 0) // frame_count
+    slot = jnp.zeros_like(wanted)
+    for i, offset in enumerate(offsets):
+        slot = jnp.where((holder ^ me) == offset, i, slot)
+    line = jnp.where(wanted >= 0, slot * frame_count + wanted % frame_count, -1)[:, None]
     phases = codes.reshape(row_count, STRIDE, books).transpose(1, 0, 2)
 
     gain = norm_gain[None, :]
-    cuts = [(0, row_count // 4, mine), (row_count // 4, row_count * 3 // 8, 0)]
-    cuts += [(row_count * 5 // 8, row_count * 3 // 8, 0)]
-    held = (tables, conv_weight)
-    partner_parts = []
-    chunks = []
-    queries = None
-    for index, (begin, rows, extra) in enumerate(cuts):
-        pieces = []
-        for phase in range(STRIDE):
-            pieces.append(phases[phase, begin : begin + rows])
-            if extra:
-                pieces.append(window_codes[lag + phase])
-        before = fetched[taps * mine :] if begin == 0 else phases[STRIDE - 1, begin - 1 : begin]
-        pieces += [before, jnp.full((PAD - 1, books), -1, jnp.int32)]
-        if extra:
-            pieces.append(window_codes[0])
-        used = STRIDE * (rows + extra) + PAD + extra
-        padded, tile = row_tiles(used)
-        if padded > used:
-            pieces.append(jnp.full((padded - used, books), -1, jnp.int32))
-        chunk_codes = jnp.concatenate(pieces, 0)
-        made = embed_conv(chunk_codes, *held, rows, extra, tile, index == 0)
-        if index == 0:
-            part, *held = made
-        else:
-            part = made
-        if extra:
-            window_parts = [part[rows:]]
-            window_parts += [swapped(part[rows:], "head", d) for d in range(1, heads_axis)]
-            queries = project(window_parts, gain, [query_weight], 0, extra, "queries")
-            part = part[:rows]
-        parts = [part] + [swapped(part, "head", d) for d in range(1, heads_axis)]
-        chunks.append(project(parts, gain, [key_weight, value_weight], 0, rows, "keys_values"))
-    all_queries, offsets = gathered(queries, "tm", stages)
-    others = [swapped(chunk, "tm", 1) for chunk in chunks]
+    early, middle = row_count // 4, row_count * 9 // 16
+    cuts = [(middle, row_count - middle), (0, early), (early, middle - early)]
+    parts = []
+    for i, cut in enumerate(cuts):
+        windows = (all_lines, line) if i == 1 else None
+        source = held if i == 2 else (tables, conv_weight)
+        part, *held = embed_conv(phases, *source, cut, windows, i < 2, i == 1)
+        parts.append([part] + [swapped(part, "head", d) for d in range(1, heads_axis)])
+
+    query = project([(parts[1], early, mine)], gain, [query_weight], "queries")
+    queries, offsets = gathered(query, "tm", stages)
+    weights = [key_weight, value_weight]
+    groups = [(part, 0, cut[1]) for part, cut in zip(parts, cuts)]
+    own = [project(some, gain, weights, "keys_values") for some in (groups[:2], groups[2:])]
+    others = [swapped(some, "tm", 1) for some in own]
 
     owners = shards // 2
-    slot_of = jnp.asarray([offsets.index(2 * i) for i in range(owners)], jnp.int32)
-    slots = slot_of[jnp.arange(owners, dtype=jnp.int32) ^ (me // 2)]
-    place = jnp.stack(
-        [me * row_count + cut[0] for cut in cuts] + [(me ^ 1) * row_count + cut[0] for cut in cuts]
-    ).astype(jnp.int32)
+    owner_of = (me // 2) ^ jnp.asarray([offset // 2 for offset in offsets], jnp.int32)
+    starts = jnp.asarray([cut[0] for cut in cuts], jnp.int32)
+    place = jnp.concatenate([me * row_count + starts, (me ^ 1) * row_count + starts])
     by_core = latent_pos.reshape(owners, 2, mine)
     latent_rows = lax.dynamic_index_in_dim(by_core, me % 2, 1, False).reshape(owners * mine, 1)
-    partials = attend(place, slots, all_queries, chunks + others, latent_rows)
-    groups = [[2 * i + core for i in range(owners)] for core in range(2)]
+    runs = [cut[1] for cut in cuts] * 2
+    partials = attend(place, owner_of, queries, own + others, runs, latent_rows)
+    same_core = [[2 * i + core for i in range(owners)] for core in range(2)]
     partials = lax.all_to_all(
-        partials, "tm", 0, 0, axis_index_groups=groups, tiled=True
+        partials, "tm", 0, 0, axis_index_groups=same_core, tiled=True
     )
     return merge(partials, owners)
 

time: 138 us -> 106 us (0.77)
  local copies, waits for them, and re-layouts: 37.1 us -> 1.65 us
  Pallas kernels: 49.1 us -> 51.6 us
  waiting for transfers between devices: 9.87 us -> 11.3 us
    unnamed x25 -> x19, local copies, waits for them, and re-layouts: 26.6 us -> 1 us
    gather x2 -> x0, local copies, waits for them, and re-layouts: 4.71 us -> none  [the longest x1 3.41 us: on_device(): fetched = jnp.take(all_codes, line, axis=0).astype(jnp.int32)]
    concatenate x8 -> x6, local copies, waits for them, and re-layouts: 4.64 us -> 0.22 us  [the longest x4 0.2 us: on_device(): jnp.concatenate([jnp.full((PAD - 1,), -1, jnp.int32), (me * frame_count -...]
    pallas_call x4, Pallas kernels: 41.5 us -> 45.1 us  [the longest x3 41.2 us: embed_conv(): pl.pallas_call(body, in_specs=[vmem] * len(operands) + [held, held], out_...]
    ppermute x16 -> x14, waiting for transfers between devices: 9.87 us -> 11.3 us  [swapped(): return lax.ppermute(value, axis, [(i, i ^ offset) for i in range(count)])]
    pallas_call x4 -> x3, Pallas kernels: 5.45 us -> 4.23 us  [project(): pl.pallas_call(body, in_specs=[vmem] * (count + 1 + len(weights)), out_sp...]
    ppermute x16 -> x14, starting transfers between devices: 18.3 us -> 17.4 us  [swapped(): return lax.ppermute(value, axis, [(i, i ^ offset) for i in range(count)])]
  transfers between devices with their start and end apart: 16 -> 14, of which waited for: 7 -> 5; matrix products, arithmetic and copies ran while one was open for 4% -> 2% of each run, Pallas kernels for 20% -> 43%
where the time goes in v2:
time: 106 us
  Pallas kernels  51.6 us (49%)
  blocking collectives  22.3 us (21%)
  starting transfers between devices  17.4 us (16%)
  waiting for transfers between devices  11.3 us (11%)
  local copies, waits for them, and re-layouts  1.65 us (2%)
  other arithmetic  1.22 us (1%)
    pallas_call x3, Pallas kernels, embed_conv(): pl.pallas_call(body, in_specs=[vmem] * len(operands) + [held, held], out_...  41.2 us
    all_to_all x1, blocking collectives, on_device(): lax.all_to_all(partials, 'tm', 0, 0, axis_index_groups=same_core, tiled=T...  22.3 us
    ppermute x14, starting transfers between devices, swapped(): return lax.ppermute(value, axis, [(i, i ^ offset) for i in range(count)])  17.4 us
    ppermute x14, waiting for transfers between devices, swapped(): return lax.ppermute(value, axis, [(i, i ^ offset) for i in range(count)])  11.3 us
    pallas_call x3, Pallas kernels, project(): pl.pallas_call(body, in_specs=[vmem] * (count + 1 + len(weights)), out_sp...  4.23 us
    pallas_call x1, Pallas kernels, attend(): pl.pallas_call(body, in_specs=[smem, smem] + [vmem] * (1 + pieces + len(k...  3.89 us
    pallas_call x1, Pallas kernels, merge(): pl.pallas_call(body, in_specs=[vmem], out_specs=vmem, out_shape=jax.Shape...  2.2 us
  transfers between devices with their start and end apart: 14, of which 5 were waited for; matrix products, arithmetic and copies ran while one was open for 2% of the time, Pallas kernels for 43%

profile of v2, /device:TPU:0, one launch (start us, length us, event | category | flops | bytes accessed | tf_op | source)
XLA Modules:
  0.0 105.8 jit_solution(5026594734388205424)
XLA Ops:
  0.0 0.8 convert_bitcast_fusion
  0.8 3.1 %collective-permute-start = (s16[8,1024]{1,0:T(8,128)(2,1)S(1)}, s16[8,1024]{1,0:T(8,128)(2,1)S(1)}, u32[]{:S(2)}, u32[]{:S(2)}) collective-permute-start(s16[8,1024]{1,0:T(8,128)(2,1)S(1)} %bitcast.29), channel_id=1, source_target_pairs={{0,8},{2,10},{4,12},{6,14},{8,0},{10,2},{12,4},{14,6},{16,24},{18,... | collective-permute-start | bytes 49160 | tf_op jit(solution)/shard_map/ppermute | solution.py:33
  3.9 2.6 %collective-permute-start.1 = (s16[8,1024]{1,0:T(8,128)(2,1)S(1)}, s16[8,1024]{1,0:T(8,128)(2,1)S(1)}, u32[]{:S(2)}, u32[]{:S(2)}) collective-permute-start(s16[8,1024]{1,0:T(8,128)(2,1)S(1)} %bitcast.30), channel_id=1, source_target_pairs={{0,16},{2,18},{4,20},{6,22},{8,24},{10,26},{12,28},{14,30},{16,0},... | collective-permute-start | bytes 49160 | tf_op jit(solution)/shard_map/ppermute | solution.py:33
  6.5 0.0 collective-permute-start.2
  6.5 1.0 copy.17
  7.5 0.0 copy-start.4
  7.5 15.3 %embed_conv.4.refs_0_ = bf16[112,2048]{1,0:T(8,128)(2,1)S(1)} custom-call(s32[4,256,8]{2,1,0:T(8,128)S(1)} %bitcast.20, bf16[8,1024,1024]{2,1,0:T(8,128)(2,1)} %refs_1_.1, bf16[5,1024,2048]{2,1,0:T(8,128)(2,1)} %refs_2_.1), custom_call_target="tpu_custom_call" | custom-call | flops 10401873920 | bytes 37748736 | tf_op jit(solution)/shard_map/embed_conv/pallas_call | solution.py:189
  22.8 1.8 %collective-permute-start.10 = (bf16[112,2048]{1,0:T(8,128)(2,1)S(1)}, bf16[112,2048]{1,0:T(8,128)(2,1)S(1)}, u32[]{:S(2)}, u32[]{:S(2)}) collective-permute-start(bf16[112,2048]{1,0:T(8,128)(2,1)S(1)} %embed_conv.4.refs_0_), channel_id=1, source_target_pairs={{0,1},{1,0},{2,3},{3,2},{4,5},{5,4},{6,7},{7,6},{8,9},{9,8},{10,11... | collective-permute-start | bytes 1376264 | tf_op jit(solution)/shard_map/ppermute | solution.py:33
  24.6 0.1 multiply_add_fusion
  24.7 0.1 concatenate.61
  24.8 0.1 broadcast_compare_fusion
  24.9 0.1 copy.21
  25.0 0.2 copy.25
  25.2 0.0 collective-permute-done.2
  25.2 1.6 %collective-permute-start.3 = (s16[32,1024]{1,0:T(8,128)(2,1)S(1)}, s16[32,1024]{1,0:T(8,128)(2,1)S(1)}, u32[]{:S(2)}, u32[]{:S(2)}) collective-permute-start(s16[32,1024]{1,0:T(8,128)(2,1)S(1)} %pad_add_fusion), channel_id=1, source_target_pairs={{0,4},{2,6},{4,0},{6,2},{8,12},{10,14},{12,8},{14,10},{16,20},{18,... | collective-permute-start | bytes 196616 | tf_op jit(solution)/shard_map/ppermute | solution.py:33
  26.8 2.7 %collective-permute-done.3 = s16[32,1024]{1,0:T(8,128)(2,1)S(1)} collective-permute-done((s16[32,1024]{1,0:T(8,128)(2,1)S(1)}, s16[32,1024]{1,0:T(8,128)(2,1)S(1)}, u32[]{:S(2)}, u32[]{:S(2)}) %collective-permute-start.3) | collective-permute-done | bytes 65568 | tf_op jit(solution)/shard_map/ppermute | solution.py:33
  29.6 0.1 collective-permute-start.4
  29.6 0.2 fusion.3.refs_2_
  29.8 1.1 %collective-permute-done.4 = s16[64,1024]{1,0:T(8,128)(2,1)S(1)} collective-permute-done((s16[64,1024]{1,0:T(8,128)(2,1)S(1)}, s16[64,1024]{1,0:T(8,128)(2,1)S(1)}, u32[]{:S(2)}, u32[]{:S(2)}) %collective-permute-start.4) | collective-permute-done | bytes 131104 | tf_op jit(solution)/shard_map/ppermute | solution.py:33
  31.0 15.6 %embed_conv.3 = (bf16[96,2048]{1,0:T(8,128)(2,1)S(1)}, bf16[8,1024,1024]{2,1,0:T(8,128)(2,1)S(1)}, bf16[5,1024,2048]{2,1,0:T(8,128)(2,1)S(1)}) custom-call(s32[4,256,8]{2,1,0:T(8,128)S(1)} %bitcast.21, s16[128,1024]{1,0:T(8,128)(2,1)S(1)} %constant_dynamic-update-slice_fusion.5.refs_1_, s32[176,1]{1,0:T(8,128)S(1)} %fusion.3.refs_2_, ...), custom_call_target="tpu_custom_call" | custom-call | flops 9529458688 | bytes 37748736 | tf_op jit(solution)/shard_map/embed_conv/pallas_call | solution.py:189
  46.6 0.4 collective-permute-start.5
  47.0 0.0 copy-start.5
  47.0 10.4 %embed_conv.5.refs_0_ = bf16[80,2048]{1,0:T(8,128)(2,1)S(1)} custom-call(s32[4,256,8]{2,1,0:T(8,128)S(1)} %bitcast.22, bf16[8,1024,1024]{2,1,0:T(8,128)(2,1)S(1)} %get-tuple-element.9.refs_1_, bf16[5,1024,2048]{2,1,0:T(8,128)(2,1)S(1)} %get-tuple-element.10.refs_2_), custom_call_target="tpu_custom_call" | custom-call | flops 7583301632 | bytes 4194304 | tf_op jit(solution)/shard_map/embed_conv/pallas_call | solution.py:189
  57.3 0.0 copy-start.6
  57.3 1.8 %collective-permute-start.11 = (bf16[80,2048]{1,0:T(8,128)(2,1)S(1)}, bf16[80,2048]{1,0:T(8,128)(2,1)S(1)}, u32[]{:S(2)}, u32[]{:S(2)}) collective-permute-start(bf16[80,2048]{1,0:T(8,128)(2,1)S(1)} %embed_conv.5.refs_0_), channel_id=1, source_target_pairs={{0,1},{1,0},{2,3},{3,2},{4,5},{5,4},{6,7},{7,6},{8,9},{9,8},{10,11... | collective-permute-start | bytes 983048 | tf_op jit(solution)/shard_map/ppermute | solution.py:33
  59.1 0.0 collective-permute-done.5.refs_1_.refs_3_
  59.1 0.8 queries.1.rest_0_
  59.9 0.7 collective-permute-start.6
  60.6 3.5 %collective-permute-start.7 = (bf16[32,1024]{1,0:T(8,128)(2,1)S(1)}, bf16[32,1024]{1,0:T(8,128)(2,1)S(1)}, u32[]{:S(2)}, u32[]{:S(2)}) collective-permute-start(bf16[32,1024]{1,0:T(8,128)(2,1)S(1)} %queries.1.rest_0_), channel_id=1, source_target_pairs={{0,16},{2,18},{4,20},{6,22},{8,24},{10,26},{12,28},{14,30},{16,0},... | collective-permute-start | bytes 196616 | tf_op jit(solution)/shard_map/ppermute | solution.py:33
  64.1 0.2 collective-permute-start.8
  64.3 0.0 collective-permute-done.10.refs_1_
  64.4 1.8 %keys_values.2.rest_5_ = bf16[176,2048]{1,0:T(8,128)(2,1)S(1)} custom-call(bf16[112,2048]{1,0:T(8,128)(2,1)S(1)} %embed_conv.4.refs_0_, bf16[112,2048]{1,0:T(8,128)(2,1)S(1)} %collective-permute-done.10.refs_1_, bf16[96,2048]{1,0:T(8,128)(2,1)S(1)} %get-tuple-element.8.refs_0_.refs_2_, bf16[96,2048]{1,0:T(8,128)(2,1)S(1)} %collective-permute-done.5.refs_1_.refs_3_, ...), custom_call_target="tpu_custom_call" | custom-call | flops 1476395008 | bytes 8388608 | tf_op jit(solution)/shard_map/keys_values/pallas_call | solution.py:243
  66.2 0.1 collective-permute-start.12
  66.3 0.6 collective-permute-done.11.refs_1_
  66.9 1.6 %keys_values.3.rest_6_ = bf16[80,2048]{1,0:T(8,128)(2,1)S(1)} custom-call(bf16[80,2048]{1,0:T(8,128)(2,1)S(1)} %embed_conv.5.refs_0_, bf16[80,2048]{1,0:T(8,128)(2,1)S(1)} %collective-permute-done.11.refs_1_, f32[1,2048]{1,0:T(1,128)S(1)} %bitcast.26, bf16[2048,1024]{1,0:T(8,128)(2,1)S(1)} %copy-done, bf16[2048,1024]{1,0:T(8,128)(2,1)S(1)} %copy-done.1), custom_call_target="tpu_custom_call" | custom-call | flops 671088640 | bytes 8388608 | tf_op jit(solution)/shard_map/keys_values/pallas_call | solution.py:243
  68.5 0.1 collective-permute-start.13
  68.6 0.0 collective-permute-done.7.rest_2_
  68.6 1.6 %collective-permute-done.8.rest_3_ = bf16[32,1024]{1,0:T(8,128)(2,1)S(1)} collective-permute-done((bf16[32,1024]{1,0:T(8,128)(2,1)S(1)}, bf16[32,1024]{1,0:T(8,128)(2,1)S(1)}, u32[]{:S(2)}, u32[]{:S(2)}) %collective-permute-start.8) | collective-permute-done | bytes 65568 | tf_op jit(solution)/shard_map/ppermute | solution.py:33
  70.2 1.6 %collective-permute-start.9 = (bf16[128,1024]{1,0:T(8,128)(2,1)S(1)}, bf16[128,1024]{1,0:T(8,128)(2,1)S(1)}, u32[]{:S(2)}, u32[]{:S(2)}) collective-permute-start(bf16[128,1024]{1,0:T(8,128)(2,1)S(1)} %pad_maximum_fusion), channel_id=1, source_target_pairs={{0,4},{2,6},{4,0},{6,2},{8,12},{10,14},{12,8},{14,10},{16,20},{18,... | collective-permute-start | bytes 786440 | tf_op jit(solution)/shard_map/ppermute | solution.py:33
  71.8 0.1 pad_add_fusion.2.place_ref
  71.9 0.1 reshape.351
  72.0 0.1 reshape.356.pos_ref
  72.1 0.0 collective-permute-done.13.rest_8_
  72.2 5.2 %collective-permute-done.9.rest_4_ = bf16[128,1024]{1,0:T(8,128)(2,1)S(1)} collective-permute-done((bf16[128,1024]{1,0:T(8,128)(2,1)S(1)}, bf16[128,1024]{1,0:T(8,128)(2,1)S(1)}, u32[]{:S(2)}, u32[]{:S(2)}) %collective-permute-start.9) | collective-permute-done | bytes 262176 | tf_op jit(solution)/shard_map/ppermute | solution.py:33
  77.4 0.0 collective-permute-done.12.rest_7_
  77.4 3.9 %attend.1 = bf16[256,1152]{1,0:T(8,128)(2,1)S(1)} custom-call(s32[6]{0:T(128)S(1)} %pad_add_fusion.2.place_ref, s32[8]{0:T(128)S(1)} %broadcast_xor_fusion.owner_ref, s32[256,1]{1,0:T(8,128)S(1)} %reshape.356.pos_ref, bf16[32,1024]{1,0:T(8,128)(2,1)S(1)} %queries.1.rest_0_, bf16[32,1024]{1,0:T(8,128)(2,1)S(1)} %collective-permute-done.6.rest_1_, ...), custom_call_target="tpu_custom_call" | custom-call | flops 536870912 | bytes 4194304 | tf_op jit(solution)/shard_map/attend/pallas_call | solution.py:312
  81.3 22.3 %all_to_all.11 = bf16[8,32,1152]{2,1,0:T(8,128)(2,1)} all-to-all(bf16[8,32,1152]{2,1,0:T(8,128)(2,1)S(1)} %bitcast.23), channel_id=1, replica_groups={{0,4,8,12,16,20,24,28},{2,6,10,14,18,22,26,30},{1,5,9,13,17,21,25,29},{..., dimensions={0} | all-to-all | bytes 1179648 | tf_op jit(solution)/shard_map/all_to_all | solution.py:416
  103.6 2.2 %merge.1 = bf16[32,1024]{1,0:T(8,128)(2,1)} custom-call(bf16[256,1152]{1,0:T(8,128)(2,1)} %bitcast.27), custom_call_target="tpu_custom_call" | custom-call | tf_op jit(solution)/shard_map/merge/pallas_call | solution.py:352
  (30 shorter events, 0.2 us)
Async XLA Ops:
  0.8 24.4 %collective-permute-start = (s16[8,1024]{1,0:T(8,128)(2,1)S(1)}, s16[8,1024]{1,0:T(8,128)(2,1)S(1)}, u32[]{:S(2)}, u32[]{:S(2)}) collective-permute-start(s16[8,1024]{1,0:T(8,128)(2,1)S(1)} %bitcast.29), channel_id=1, source_target_pairs={{0,8},{2,10},{4,12},{6,14},{8,0},{10,2},{12,4},{14,6},{16,24},{18,... | collective-permute-start | bytes 49160 | tf_op jit(solution)/shard_map/ppermute | solution.py:33
  3.9 21.3 %collective-permute-start.1 = (s16[8,1024]{1,0:T(8,128)(2,1)S(1)}, s16[8,1024]{1,0:T(8,128)(2,1)S(1)}, u32[]{:S(2)}, u32[]{:S(2)}) collective-permute-start(s16[8,1024]{1,0:T(8,128)(2,1)S(1)} %bitcast.30), channel_id=1, source_target_pairs={{0,16},{2,18},{4,20},{6,22},{8,24},{10,26},{12,28},{14,30},{16,0},... | collective-permute-start | bytes 49160 | tf_op jit(solution)/shard_map/ppermute | solution.py:33
  6.5 18.7 %collective-permute-start.2 = (s16[8,1024]{1,0:T(8,128)(2,1)S(1)}, s16[8,1024]{1,0:T(8,128)(2,1)S(1)}, u32[]{:S(2)}, u32[]{:S(2)}) collective-permute-start(s16[8,1024]{1,0:T(8,128)(2,1)S(1)} %bitcast.31), channel_id=1, source_target_pairs={{0,24},{2,26},{4,28},{6,30},{8,16},{10,18},{12,20},{14,22},{16,8},... | collective-permute-start | bytes 49160 | tf_op jit(solution)/shard_map/ppermute | solution.py:33
  7.5 17.1 %copy-start.4 = (s32[512]{0:T(512)S(1)}, s32[512]{0:T(512)}, u32[]{:S(2)}) copy-start(s32[512]{0:T(512)} %param.17) | copy-start | bytes 6148
  22.8 41.5 %collective-permute-start.10 = (bf16[112,2048]{1,0:T(8,128)(2,1)S(1)}, bf16[112,2048]{1,0:T(8,128)(2,1)S(1)}, u32[]{:S(2)}, u32[]{:S(2)}) collective-permute-start(bf16[112,2048]{1,0:T(8,128)(2,1)S(1)} %embed_conv.4.refs_0_), channel_id=1, source_target_pairs={{0,1},{1,0},{2,3},{3,2},{4,5},{5,4},{6,7},{7,6},{8,9},{9,8},{10,11... | collective-permute-start | bytes 1376264 | tf_op jit(solution)/shard_map/ppermute | solution.py:33
  25.2 4.3 %collective-permute-start.3 = (s16[32,1024]{1,0:T(8,128)(2,1)S(1)}, s16[32,1024]{1,0:T(8,128)(2,1)S(1)}, u32[]{:S(2)}, u32[]{:S(2)}) collective-permute-start(s16[32,1024]{1,0:T(8,128)(2,1)S(1)} %pad_add_fusion), channel_id=1, source_target_pairs={{0,4},{2,6},{4,0},{6,2},{8,12},{10,14},{12,8},{14,10},{16,20},{18,... | collective-permute-start | bytes 196616 | tf_op jit(solution)/shard_map/ppermute | solution.py:33
  29.6 1.4 %collective-permute-start.4 = (s16[64,1024]{1,0:T(8,128)(2,1)S(1)}, s16[64,1024]{1,0:T(8,128)(2,1)S(1)}, u32[]{:S(2)}, u32[]{:S(2)}) collective-permute-start(s16[64,1024]{1,0:T(8,128)(2,1)S(1)} %get-tuple-element.13), channel_id=1, source_target_pairs={{0,2},{2,0},{4,6},{6,4},{8,10},{10,8},{12,14},{14,12},{16,18},{18,... | collective-permute-start | bytes 393224 | tf_op jit(solution)/shard_map/ppermute | solution.py:33
  46.6 12.5 %collective-permute-start.5 = (bf16[96,2048]{1,0:T(8,128)(2,1)S(1)}, bf16[96,2048]{1,0:T(8,128)(2,1)S(1)}, u32[]{:S(2)}, u32[]{:S(2)}) collective-permute-start(bf16[96,2048]{1,0:T(8,128)(2,1)S(1)} %get-tuple-element.8.refs_0_.refs_2_), channel_id=1, source_target_pairs={{0,1},{1,0},{2,3},{3,2},{4,5},{5,4},{6,7},{7,6},{8,9},{9,8},{10,11... | collective-permute-start | bytes 1179656 | tf_op jit(solution)/shard_map/ppermute | solution.py:33
  46.9 12.2 %copy-start.2 = (bf16[2048,1024]{1,0:T(8,128)(2,1)S(1)}, bf16[2048,1024]{1,0:T(8,128)(2,1)}, u32[]{:S(2)}) copy-start(bf16[2048,1024]{1,0:T(8,128)(2,1)} %refs_3_.4) | copy-start | bytes 12582916
  46.9 12.2 %copy-start.3 = (f32[2048]{0:T(1024)S(1)}, f32[2048]{0:T(1024)}, u32[]{:S(2)}) copy-start(f32[2048]{0:T(1024)} %param.13) | copy-start | bytes 24580
  46.9 17.4 %copy-start = (bf16[2048,1024]{1,0:T(8,128)(2,1)S(1)}, bf16[2048,1024]{1,0:T(8,128)(2,1)}, u32[]{:S(2)}) copy-start(bf16[2048,1024]{1,0:T(8,128)(2,1)} %refs_3_.5) | copy-start | bytes 12582916
  46.9 17.4 %copy-start.1 = (bf16[2048,1024]{1,0:T(8,128)(2,1)S(1)}, bf16[2048,1024]{1,0:T(8,128)(2,1)}, u32[]{:S(2)}) copy-start(bf16[2048,1024]{1,0:T(8,128)(2,1)} %refs_4_.3) | copy-start | bytes 12582916
  47.0 19.3 %copy-start.5 = (s32[3]{0:T(128)S(1)}, s32[3]{0:T(128)}, u32[]{:S(2)}) copy-start(s32[3]{0:T(128)} %constant.122.clone) | copy-start | bytes 40
  57.3 14.8 %copy-start.6 = (s32[8]{0:T(128)S(1)}, s32[8]{0:T(128)}, u32[]{:S(2)}) copy-start(s32[8]{0:T(128)} %constant.121.clone) | copy-start | bytes 100
  57.3 9.6 %collective-permute-start.11 = (bf16[80,2048]{1,0:T(8,128)(2,1)S(1)}, bf16[80,2048]{1,0:T(8,128)(2,1)S(1)}, u32[]{:S(2)}, u32[]{:S(2)}) collective-permute-start(bf16[80,2048]{1,0:T(8,128)(2,1)S(1)} %embed_conv.5.refs_0_), channel_id=1, source_target_pairs={{0,1},{1,0},{2,3},{3,2},{4,5},{5,4},{6,7},{7,6},{8,9},{9,8},{10,11... | collective-permute-start | bytes 983048 | tf_op jit(solution)/shard_map/ppermute | solution.py:33
  59.9 8.6 %collective-permute-start.6 = (bf16[32,1024]{1,0:T(8,128)(2,1)S(1)}, bf16[32,1024]{1,0:T(8,128)(2,1)S(1)}, u32[]{:S(2)}, u32[]{:S(2)}) collective-permute-start(bf16[32,1024]{1,0:T(8,128)(2,1)S(1)} %queries.1.rest_0_), channel_id=1, source_target_pairs={{0,8},{2,10},{4,12},{6,14},{8,0},{10,2},{12,4},{14,6},{16,24},{18,... | collective-permute-start | bytes 196616 | tf_op jit(solution)/shard_map/ppermute | solution.py:33
  60.6 8.0 %collective-permute-start.7 = (bf16[32,1024]{1,0:T(8,128)(2,1)S(1)}, bf16[32,1024]{1,0:T(8,128)(2,1)S(1)}, u32[]{:S(2)}, u32[]{:S(2)}) collective-permute-start(bf16[32,1024]{1,0:T(8,128)(2,1)S(1)} %queries.1.rest_0_), channel_id=1, source_target_pairs={{0,16},{2,18},{4,20},{6,22},{8,24},{10,26},{12,28},{14,30},{16,0},... | collective-permute-start | bytes 196616 | tf_op jit(solution)/shard_map/ppermute | solution.py:33
  64.1 6.1 %collective-permute-start.8 = (bf16[32,1024]{1,0:T(8,128)(2,1)S(1)}, bf16[32,1024]{1,0:T(8,128)(2,1)S(1)}, u32[]{:S(2)}, u32[]{:S(2)}) collective-permute-start(bf16[32,1024]{1,0:T(8,128)(2,1)S(1)} %queries.1.rest_0_), channel_id=1, source_target_pairs={{0,24},{2,26},{4,28},{6,30},{8,16},{10,18},{12,20},{14,22},{16,8},... | collective-permute-start | bytes 196616 | tf_op jit(solution)/shard_map/ppermute | solution.py:33
  66.2 11.2 %collective-permute-start.12 = (bf16[176,2048]{1,0:T(8,128)(2,1)S(1)}, bf16[176,2048]{1,0:T(8,128)(2,1)S(1)}, u32[]{:S(2)}, u32[]{:S(2)}) collective-permute-start(bf16[176,2048]{1,0:T(8,128)(2,1)S(1)} %keys_values.2.rest_5_), channel_id=1, source_target_pairs={{0,2},{2,0},{4,6},{6,4},{8,10},{10,8},{12,14},{14,12},{16,18},{18,... | collective-permute-start | bytes 2162696 | tf_op jit(solution)/shard_map/ppermute | solution.py:33
  68.5 3.7 %collective-permute-start.13 = (bf16[80,2048]{1,0:T(8,128)(2,1)S(1)}, bf16[80,2048]{1,0:T(8,128)(2,1)S(1)}, u32[]{:S(2)}, u32[]{:S(2)}) collective-permute-start(bf16[80,2048]{1,0:T(8,128)(2,1)S(1)} %keys_values.3.rest_6_), channel_id=1, source_target_pairs={{0,2},{2,0},{4,6},{6,4},{8,10},{10,8},{12,14},{14,12},{16,18},{18,... | collective-permute-start | bytes 983048 | tf_op jit(solution)/shard_map/ppermute | solution.py:33
  70.2 7.2 %collective-permute-start.9 = (bf16[128,1024]{1,0:T(8,128)(2,1)S(1)}, bf16[128,1024]{1,0:T(8,128)(2,1)S(1)}, u32[]{:S(2)}, u32[]{:S(2)}) collective-permute-start(bf16[128,1024]{1,0:T(8,128)(2,1)S(1)} %pad_maximum_fusion), channel_id=1, source_target_pairs={{0,4},{2,6},{4,0},{6,2},{8,12},{10,14},{12,8},{14,10},{16,20},{18,... | collective-permute-start | bytes 786440 | tf_op jit(solution)/shard_map/ppermute | solution.py:33
